TPU v7x, 256 devices: a whole 4x4x8 slice. The times are simulated.
256 devices in a mesh: dp: 8 (over x, core), expert: 32 (over z, y).
Axes of the slice: x: 4, y: 4, z: 8, core: 2. Of those that a mesh axis runs over, the one named last changes fastest.
Arguments:
- tokens: bfloat16 [32768, 1024], P(('dp', 'expert')), may hold values from -6 to 6
- router: float32 [1024, 32], replicated, may hold values from -0.1875 to 0.1875
- expert_lists: int32 [32768, 4], P(('dp', 'expert')), may hold values from 0 to 31, as said below
- slot_positions: int32 [32768, 4], P(('dp', 'expert')), may hold values from 0 to 19, as said below
- teacher_gate: bfloat16 [1024, 2752], P(None, 'expert'), may hold values from -0.1875 to 0.1875
- teacher_up: bfloat16 [1024, 2752], P(None, 'expert'), may hold values from -0.1875 to 0.1875
- teacher_down: bfloat16 [2752, 1024], P('expert'), may hold values from -0.109375 to 0.109375
- expert_gate: bfloat16 [32, 1024, 704], P('expert'), may hold values from -0.1875 to 0.1875
- expert_up: bfloat16 [32, 1024, 704], P('expert'), may hold values from -0.1875 to 0.1875
- expert_down: bfloat16 [32, 704, 1024], P('expert'), may hold values from -0.21875 to 0.21875
Outputs:
- grad_gate: float32 [32, 1024, 704], P('expert', 'dp')
- grad_up: float32 [32, 1024, 704], P('expert', 'dp')
- grad_down: float32 [32, 704, 1024], P('expert', None, 'dp')
Inputs may be any that keep to these rules, and one draw needn't show every extreme that they name: `expert_lists`: the k-th expert of every token lies among k * 8 to (k + 1) * 8 - 1. The tokens of one device name each expert at most 20 times. For each index of dp and each such quarter of the experts, one expert is named exactly 20 times by the tokens of every device of that index. `slot_positions`: copies from the tokens of one device that name the same expert have distinct slots.
All inputs are finite; a program needn't handle non-finite values.
Results may differ from a plain program's by a relative error of at most 0.015.
Values may be sent and summed in bfloat16 or wider, within the bound.
No kernel may reach another device: no remote copies, remote signals or barrier semaphores. Data moves between devices by JAX's collectives and lax.ppermute only.
A program may use at most 128 MiB of HBM per device.

v0:
```python
import functools
import math

import jax
import jax.numpy as jnp
from jax import lax
from jax.experimental import pallas as pl
from jax.experimental.pallas import tpu as pltpu
from jax.sharding import Mesh, PartitionSpec as P


BF16 = jnp.bfloat16
F32 = jnp.float32
ALL = ("x", "core", "zq", "zp", "y")
DP = ("x", "core")
EXPERT = ("zq", "zp", "y")
VMEM = pl.BlockSpec(memory_space=pltpu.VMEM)
HBM = pl.BlockSpec(memory_space=pltpu.MemorySpace.HBM)
GRANT_D, GRANT_F, GRANT_G = 62, 49, 24
STEP = 24


def call(body, outs, args, specs=None, out_specs=None, scratch=(), flops=0, grant=24):
    moved = sum(a.size * a.dtype.itemsize for a in args)
    moved += sum(math.prod(o.shape) * o.dtype.itemsize for o in outs)
    return pl.pallas_call(
        body,
        out_shape=tuple(outs),
        in_specs=specs or [VMEM] * len(args),
        out_specs=tuple(out_specs or [VMEM] * len(outs)),
        scratch_shapes=list(scratch),
        cost_estimate=pl.CostEstimate(flops=flops, bytes_accessed=moved, transcendentals=0),
        compiler_params=pltpu.CompilerParams(vmem_limit_bytes=grant * 1024 * 1024),
    )(*args)


def shape(dims, dtype):
    return jax.ShapeDtypeStruct(dims, dtype)


def nt(a, b):
    return lax.dot_general(a, b, (((1,), (1,)), ((), ())), preferred_element_type=F32)


def tn(a, b):
    return lax.dot_general(a, b, (((0,), (0,)), ((), ())), preferred_element_type=F32)


def nn(a, b):
    return jnp.dot(a, b, preferred_element_type=F32)


def sigmoid(v):
    return 1.0 / (1.0 + jnp.exp(-v))


def split(v):
    high = v.astype(BF16)
    return high, (v - high.astype(F32)).astype(BF16)


def as_bf16(mask):
    return jnp.where(mask, 1.0, 0.0).astype(BF16)


def iota(dims, axis):
    return lax.broadcasted_iota(jnp.int32, dims, axis)


def fetch(pairs, sems):
    copies = [pltpu.make_async_copy(src, dst, sems.at[i]) for i, (src, dst) in enumerate(pairs)]
    for copy in copies:
        copy.start()
    return copies


def quotient(v, by):
    return ((v.astype(F32) + 0.5) * (1.0 / by)).astype(jnp.int32)


def dispatch_body(
    cap, tok_h, router_h, lists_h, slots_h, gate_h, up_h, down_h, send, weights, shard,
    tok, router, lists, slots, gate, up, down, ext, sems,
):
    copies = fetch(
        [(router_h, router), (tok_h, tok), (lists_h, lists), (slots_h, slots)]
        + [(gate_h, gate), (up_h, up), (down_h, down)],
        sems,
    )
    for copy in copies[:4]:
        copy.wait()
    experts, count = router.shape[0], tok.shape[0]
    top = lists.shape[0]
    rows = experts * STEP
    logits = lax.dot_general(
        router[...],
        tok[...].astype(F32),
        (((1,), (1,)), ((), ())),
        precision=lax.Precision.HIGHEST,
        preferred_element_type=F32,
    )
    which = iota((experts, count), 0)
    picked = [
        jnp.sum(jnp.where(which == lists[k : k + 1, :], logits, 0.0), axis=0, keepdims=True)
        for k in range(top)
    ]
    gates = [sigmoid(p) for p in picked]
    total = functools.reduce(jnp.add, gates)
    parts = [g / total for g in gates]
    for k in range(top):
        weights[k : k + 1, :] = parts[k]
    spread = jnp.concatenate(
        [jnp.where(which == lists[k : k + 1, :], parts[k], 0.0) for k in range(top)], axis=1
    )
    high, low = split(spread)
    slot = iota((128, count), 0)
    place = jnp.concatenate([as_bf16(slot == slots[k : k + 1, :]) for k in range(top)], axis=1)
    ext[0:count, :] = tok[...]
    ext[count:, :] = jnp.zeros((ext.shape[0] - count, ext.shape[1]), BF16)
    ext[count : count + experts, 0:128] = nt(high, place).astype(BF16)
    ext[count : count + experts, 128:256] = nt(low, place).astype(BF16)
    row = iota((rows, count), 0)
    hit = functools.reduce(
        jnp.logical_or,
        [row == lists[k : k + 1, :] * STEP + slots[k : k + 1, :] for k in range(top)],
    )
    extra = row == iota((rows, count), 1) * STEP + cap
    onehot = jnp.concatenate([as_bf16(hit), as_bf16(extra)], axis=1)
    send[...] = nn(onehot, ext[...]).astype(BF16)
    for copy in copies[4:]:
        copy.wait()
    core = lax.axis_index("core")
    cut = shard.shape[0] // 3
    for i, piece in enumerate((gate, up, down)):
        units = piece.shape[0]
        at = i * cut
        full = (units - cut) // 16 * 16

        @pl.when(core == 0)
        def _(piece=piece, at=at):
            shard[at : at + cut, :] = piece[0:cut, :]

        @pl.when(core != 0)
        def _(piece=piece, at=at, full=full, units=units):
            shard[at : at + full, :] = piece[cut : cut + full, :]
            shard[at + full : at + cut, :] = jnp.zeros((cut - full, shard.shape[1]), BF16)
            shard[at + full : at + units - cut, :] = piece[cut + full : units, :]


def packing(cap, flip):
    dims = (8 * STEP, 8 * cap) if flip else (8 * cap, 8 * STEP)
    wire, wide = iota(dims, 1 if flip else 0), iota(dims, 0 if flip else 1)
    part = quotient(wire, cap)
    block = quotient(wire, 2 * cap)
    half = part - 2 * block
    return as_bf16(wide == half * (4 * STEP) + block * STEP + wire - part * cap)


def forward_body(
    cap, recv, gate, up, down_h, own_h, other_h, rows, pre_gate, pre_up, ret,
    down, own, other, x_out, g_out, u_out, sems,
):
    copies = fetch([(down_h, down), (own_h, own), (other_h, other)], sems)
    count, model = recv.shape

    def save(src, dst, at):
        copy = pltpu.make_async_copy(src, dst, sems.at[at])
        copy.start()
        return copy

    experts = count // STEP
    line = iota((count, 128), 0)
    slot = line - quotient(line, STEP) * STEP
    keep = as_bf16(slot < cap)
    x = recv[...] * jnp.concatenate([keep] * (model // 128), axis=1)
    x_out[...] = x
    saves = [save(x_out, rows, 3)]
    pick = as_bf16(iota((experts, count), 1) == iota((experts, count), 0) * STEP + cap)
    found = nn(pick, recv[:, 0:256]).astype(BF16)
    row = iota((count, experts), 0)
    first = iota((count, experts), 1) * STEP
    spread = as_bf16(jnp.logical_and(row >= first, row < first + STEP))
    wide = nn(spread, found)
    wide = wide[:, 0:128] + wide[:, 128:256]
    mine = jnp.logical_and(iota((count, 128), 1) == slot, slot < cap)
    weight = jnp.sum(jnp.where(mine, wide, 0.0), axis=1, keepdims=True)
    g = nt(gate[...], x)
    g_out[...] = g
    saves.append(save(g_out, pre_gate, 4))
    u = nt(up[...], x)
    u_out[...] = u
    saves.append(save(u_out, pre_up, 5))
    hidden = (g * sigmoid(g) * u).astype(BF16)
    copies[0].wait()
    acc = weight * tn(hidden, down[...])
    for copy, piece in zip(copies[1:], (own, other)):
        units = piece.shape[1] // 3
        take = lambda i: piece[:, i * units : (i + 1) * units, :].reshape(-1, model)
        copy.wait()
        a = nt(take(0), x)
        b = nt(take(1), x)
        hidden = (a * sigmoid(a) * b).astype(BF16)
        acc = acc - tn(hidden, take(2))
    result = acc.astype(BF16)
    pack = packing(cap, False)
    tall = 4 * STEP
    for i in range(experts // 4):
        part = result[i * tall : (i + 1) * tall, :]
        both = jnp.concatenate([part[:, : model // 2], part[:, model // 2 :]], axis=0)
        ret[i * 8 * cap : (i + 1) * 8 * cap, :] = nn(pack, both).astype(BF16)
    for copy in saves:
        copy.wait()


def error_body(cap, scale, ret, weights, lists_h, slots_h, send, lists, slots, sems):
    copies = fetch([(lists_h, lists), (slots_h, slots)], sems)
    top, count = lists.shape
    rows, half_width = ret.shape
    row = iota((rows, count), 0)
    part = quotient(row, cap)
    half = jnp.bitwise_and(part, 1)
    key = row - cap * half
    left = half == 0
    for copy in copies:
        copy.wait()
    hits = [key == lists[k : k + 1, :] * (2 * cap) + slots[k : k + 1, :] for k in range(top)]
    hit = functools.reduce(jnp.logical_or, hits)
    value = ret[...]
    error = scale * jnp.concatenate(
        [
            tn(as_bf16(jnp.logical_and(hit, left)), value),
            tn(as_bf16(jnp.logical_and(hit, jnp.logical_not(left))), value),
        ],
        axis=1,
    )
    high, low = split(error)
    spread = functools.reduce(
        jnp.add, [jnp.where(hits[k], weights[k : k + 1, :], 0.0) for k in range(top)]
    )
    w_high, w_low = split(spread)
    lhs = jnp.concatenate([w_high, w_high, w_low], axis=1)
    rhs = jnp.concatenate([high, low, high], axis=0)
    side = jnp.concatenate([left] * (half_width // count), axis=1)
    send[...] = jnp.where(
        side, nn(lhs, rhs[:, :half_width]), nn(lhs, rhs[:, half_width:])
    ).astype(BF16)


def chunk(parts, rows, cot, rels, puts):
    core, x_at = lax.axis_index("core"), lax.axis_index("x")

    def columns(ref):
        pieces = []
        for rel in rels:
            first = pl.multiple_of(jnp.bitwise_and(x_at + rel, 3) * 256, 256)
            pieces.append(ref[:, pl.ds(first, 256)])
        return jnp.concatenate(pieces, axis=1)

    side = columns(rows)
    width = parts[0].shape[0]
    for i, part in enumerate(parts):
        value = nn(part, columns(cot) if i == 2 else side).astype(BF16)
        at = slice(i * width, (i + 1) * width)
        for j, (mine, theirs) in enumerate(puts):
            left = value[:, j * 256 : j * 256 + 128]
            right = value[:, j * 256 + 128 : (j + 1) * 256]

            @pl.when(core == 0)
            def _(left=left, right=right, at=at, mine=mine, theirs=theirs):
                mine(at, left)
                theirs(at, right)

            @pl.when(core != 0)
            def _(left=left, right=right, at=at, mine=mine, theirs=theirs):
                mine(at, right)
                theirs(at, left)


def putter(ref, at=None):
    def put(rows, value):
        if at is None:
            ref[rows, :] = value
        else:
            ref[at, rows, :] = value

    return put


def grad_body(cap, wire, rows, pre_gate, pre_up, down, d_gate, d_up, hidden, cot, mine, theirs):
    count, model = cot.shape
    unpack = packing(cap, True)
    tall = 4 * STEP
    for i in range(count // tall):
        both = nn(unpack, wire[i * 8 * cap : (i + 1) * 8 * cap, :]).astype(BF16)
        cot[i * tall : (i + 1) * tall, : model // 2] = both[:tall]
        cot[i * tall : (i + 1) * tall, model // 2 :] = both[tall:]
    grad_hidden = nt(down[...], cot[...])
    g = pre_gate[...]
    u = pre_up[...]
    s = sigmoid(g)
    act = g * s
    parts = (
        (grad_hidden * u * s * (1.0 + g * (1.0 - s))).astype(BF16),
        (grad_hidden * act).astype(BF16),
        (act * u).astype(BF16),
    )
    for ref, value in zip((d_gate, d_up, hidden), parts):
        ref[...] = value
    chunk(parts, rows, cot, (2,), [(putter(mine), putter(theirs))])


def near_body(d_gate, d_up, hidden, rows, cot, mine, theirs):
    parts = (d_gate[...], d_up[...], hidden[...])
    puts = [(putter(mine, at), putter(theirs, at)) for at in range(2)]
    chunk(parts, rows, cot, (1, 3), puts)


def own_body(d_gate, d_up, hidden, rows, cot, mine, theirs):
    parts = (d_gate[...], d_up[...], hidden[...])
    chunk(parts, rows, cot, (0,), [(putter(mine), putter(theirs))])


def plus(a, b):
    return (a.astype(F32) + b.astype(F32)).astype(BF16)


def far_body(mine, got, up, down):
    half = up.shape[0]
    up[...] = plus(mine[:half, :], got[:half, :])
    down[...] = plus(mine[half:, :], got[half:, :])


def fold_body(mine, got, up_late, up_now, down_now, down_late):
    half = up_late.shape[0]
    up_late[...] = plus(mine[0, :half, :], got[0, :half, :])
    up_now[...] = plus(mine[0, half:, :], got[0, half:, :])
    down_now[...] = plus(mine[1, :half, :], got[1, :half, :])
    down_late[...] = plus(mine[1, half:, :], got[1, half:, :])


def add_body(a, b, c, d, first, second):
    first[...] = plus(a[...], b[...])
    second[...] = plus(c[...], d[...])


def finish_body(mine, got, up_late, up_now, down_now, down_late, *outs):
    half = up_late.shape[0]
    add = lambda *values: functools.reduce(jnp.add, [v.astype(F32) for v in values])
    low = add(mine[:half, :], got[:half, :], up_late[...], down_now[...])
    high = add(mine[half:, :], got[half:, :], up_now[...], down_late[...])
    width = outs[0].shape[0]
    outs[0][...] = low[0:width]
    outs[1][0 : half - width, :] = low[width:]
    outs[1][half - width :, :] = high[0 : 2 * width - half]
    outs[2][...] = high[2 * width - half :]


def on_device(tokens, router, lists, slots, t_gate, t_up, t_down, e_gate, e_up, e_down):
    count, model = tokens.shape
    top = lists.shape[1]
    experts = router.shape[1]
    width = e_gate.shape[2]
    cap = 5 * count // experts
    rows = experts * STEP
    scale = top / math.sqrt(count * 256 * top / experts)
    cut = 48
    lists_t, slots_t = lists.T, slots.T
    shards = [t_gate.T, t_up.T, t_down]
    send, weights, shard = call(
        functools.partial(dispatch_body, cap),
        [shape((rows, model), BF16), shape((top, count), F32), shape((3 * cut, model), BF16)],
        [tokens, router.T, lists_t, slots_t] + shards,
        specs=[HBM] * 7,
        scratch=[
            pltpu.VMEM((count, model), BF16),
            pltpu.VMEM((experts, model), F32),
            pltpu.VMEM((top, count), jnp.int32),
            pltpu.VMEM((top, count), jnp.int32),
        ]
        + [pltpu.VMEM(t.shape, BF16) for t in shards]
        + [pltpu.VMEM((2 * count, model), BF16), pltpu.SemaphoreType.DMA((7,))],
        flops=2 * rows * 256 * model,
        grant=GRANT_D,
    )

    def shift(v, axis, size, by):
        return lax.ppermute(v, axis, [(s, (s + by) % size) for s in range(size)])

    pair = shift(shard, "zp", 2, 1)
    after = shift(shard, "y", 4, 1)
    before = shift(shard, "y", 4, -1)
    pair_after = shift(pair, "y", 4, 1)
    pair_before = shift(pair, "y", 4, -1)
    far = shift(after, "y", 4, 1)
    pair_far = shift(pair_before, "y", 4, -1)
    gathered = jnp.stack(
        [shard, pair, after, before, pair_after, pair_before, far, pair_far], axis=0
    )

    def exchange(v):
        v = v.reshape(experts, -1, v.shape[1])
        out = lax.all_to_all(v, EXPERT, 0, 0, tiled=True)
        return out.reshape(-1, v.shape[2])

    recv = exchange(send)
    gate_t, up_t, down = e_gate[0].T, e_up[0].T, e_down[0]
    weight_buf = pltpu.VMEM((width, model), BF16)
    swap = [(0, 1), (1, 0)]
    other = lax.ppermute(gathered, "core", swap)
    piece_buf = pltpu.VMEM(gathered.shape, BF16)
    x, pre_gate, pre_up, ret = call(
        functools.partial(forward_body, cap),
        [shape((rows, model), BF16), shape((width, rows), F32), shape((width, rows), F32)]
        + [shape((2 * experts * cap, model // 2), BF16)],
        [recv, gate_t, up_t, down, gathered, other],
        specs=[VMEM] * 3 + [HBM] * 3,
        out_specs=[HBM, HBM, HBM, VMEM],
        scratch=[weight_buf]
        + [piece_buf] * 2
        + [pltpu.VMEM((rows, model), BF16)]
        + [pltpu.VMEM((width, rows), F32)] * 2
        + [pltpu.SemaphoreType.DMA((6,))],
        flops=6 * rows * (width + 768) * model,
        grant=GRANT_F,
    )
    index_buf = pltpu.VMEM((top, count), jnp.int32)
    (cot_send,) = call(
        functools.partial(error_body, cap, scale),
        [shape((2 * experts * cap, model // 2), BF16)],
        [exchange(ret), weights, lists_t, slots_t],
        specs=[VMEM, VMEM, HBM, HBM],
        scratch=[index_buf] * 2 + [pltpu.SemaphoreType.DMA((2,))],
        flops=2 * rows * 512 * model,
    )
    tall = 3 * width
    side = shape((width, rows), BF16)
    one, two = shape((tall, 128), BF16), shape((2, tall, 128), BF16)
    d_gate, d_up, hidden, cot, far_mine, far_theirs = call(
        functools.partial(grad_body, cap),
        [side] * 3 + [shape((rows, model), BF16)] + [one] * 2,
        [exchange(cot_send), x, pre_gate, pre_up, down],
        flops=4 * rows * width * model,
        grant=GRANT_G,
    )
    far_got = lax.ppermute(far_theirs, "core", swap)
    parts = [d_gate, d_up, hidden, x, cot]
    mine, theirs = call(near_body, [two] * 2, parts, flops=3 * rows * width * model, grant=GRANT_G)
    got = lax.ppermute(theirs, "core", swap)
    half = tall // 2
    halves = shape((half, 128), BF16)
    up = [(s, (s + 1) % 4) for s in range(4)]
    dn = [(s, (s - 1) % 4) for s in range(4)]
    far_up, far_down = call(far_body, [halves] * 2, [far_mine, far_got])
    a = lax.ppermute(far_up, "x", up)
    b = lax.ppermute(far_down, "x", dn)
    up_late, up_now, down_now, down_late = call(fold_body, [halves] * 4, [mine, got])
    now_up = lax.ppermute(up_now, "x", up)
    now_dn = lax.ppermute(down_now, "x", dn)
    own_mine, own_theirs = call(
        own_body, [one] * 2, parts, flops=3 * rows * width * model // 2, grant=GRANT_G
    )
    own_got = lax.ppermute(own_theirs, "core", swap)
    late_up, late_dn = call(add_body, [halves] * 2, [up_late, a, down_late, b])
    late_up = lax.ppermute(late_up, "x", up)
    late_dn = lax.ppermute(late_dn, "x", dn)
    g, u, d = call(
        finish_body,
        [shape((width, 128), F32)] * 3,
        [own_mine, own_got, late_up, now_up, now_dn, late_dn],
    )
    return g.T[None], u.T[None], d[None]


def solution(mesh):
    fine = Mesh(mesh.devices.reshape(4, 2, 4, 2, 4), ALL)

    return jax.shard_map(
        on_device,
        mesh=fine,
        in_specs=(
            P(ALL, None),
            P(),
            P(ALL, None),
            P(ALL, None),
            P(None, EXPERT),
            P(None, EXPERT),
            P(EXPERT, None),
            P(EXPERT, None, None),
            P(EXPERT, None, None),
            P(EXPERT, None, None),
        ),
        out_specs=(P(EXPERT, DP, None), P(EXPERT, DP, None), P(EXPERT, None, DP)),
        check_vma=False,
    )
```

profile of v0, /device:TPU:8, one launch (start us, length us, event | category | flops | bytes accessed | tf_op | source)
XLA Modules:
  0.0 190.3 jit_solution(142618149992460518)
XLA Ops:
  0.6 4.5 %shard_map.121 = (bf16[768,1024]{1,0:T(8,128)(2,1)}, f32[4,128]{1,0:T(4,128)}, bf16[144,1024]{1,0:T(8,128)(2,1)}) custom-call(bf16[128,1024]{1,0:T(8,128)(2,1)} %tok_h.1, f32[32,1024]{1,0:T(8,128)} %bitcast.59, s32[4,128]{1,0:T(4,128)} %bitcast.49, s32[4,128]{1,0:T(4,128)} %bitcast.51, bf16[86,1024]{1,0:T(8,128)(2,1)} %bitcast.57, ...), custom_call_target="tpu_custom_call" | custom-call | flops 402653184 | bytes 2795520 | tf_op jit(solution)/shard_map/pallas_call | solution.py:26
  5.1 2.0 %collective-permute-start = (bf16[144,1024]{1,0:T(8,128)(2,1)}, bf16[144,1024]{1,0:T(8,128)(2,1)S(1)}, u32[]{:S(2)}, u32[]{:S(2)}) collective-permute-start(bf16[144,1024]{1,0:T(8,128)(2,1)} %get-tuple-element.32), channel_id=1, source_target_pairs={{0,4},{4,0},{1,5},{5,1},{2,6},{6,2},{3,7},{7,3},{8,12},{12,8},{9,1... | collective-permute-start | bytes 884744 | tf_op jit(solution)/shard_map/ppermute | solution.py:387
  9.2 10.8 %all-to-all-start = ((bf16[32,24,1024]{2,1,0:T(8,128)(2,1)}), bf16[32,24,1024]{2,1,0:T(8,128)(2,1)}, u32[]{:S(2)}, u32[]{:S(2)}) async-start(bf16[32,24,1024]{2,1,0:T(8,128)(2,1)} %bitcast.53), calls=%async_computation | async-start | bytes 3145728 | tf_op jit(solution)/shard_map/all_to_all | solution.py:402
  20.1 1.9 bitcast_dynamic-update-slice_fusion.7
  22.2 1.7 collective-permute-start.3
  28.6 7.7 %collective-permute-done.4 = bf16[144,1024]{1,0:T(8,128)(2,1)S(1)} collective-permute-done((bf16[144,1024]{1,0:T(8,128)(2,1)S(1)}, bf16[144,1024]{1,0:T(8,128)(2,1)S(1)}, u32[]{:S(2)}, u32[]{:S(2)}) %collective-permute-start.4) | collective-permute-done | bytes 294944 | tf_op jit(solution)/shard_map/ppermute | solution.py:387
  36.3 1.9 %collective-permute-start.6 = (bf16[144,1024]{1,0:T(8,128)(2,1)S(1)}, bf16[144,1024]{1,0:T(8,128)(2,1)S(1)}, u32[]{:S(2)}, u32[]{:S(2)}) collective-permute-start(bf16[144,1024]{1,0:T(8,128)(2,1)S(1)} %collective-permute-done.4), channel_id=1, source_target_pairs={{0,3},{1,0},{2,1},{3,2},{4,7},{5,4},{6,5},{7,6},{8,11},{9,8},{10,9... | collective-permute-start | bytes 884744 | tf_op jit(solution)/shard_map/ppermute | solution.py:387
  39.7 6.9 %collective-permute-done.5 = bf16[144,1024]{1,0:T(8,128)(2,1)S(1)} collective-permute-done((bf16[144,1024]{1,0:T(8,128)(2,1)S(1)}, bf16[144,1024]{1,0:T(8,128)(2,1)S(1)}, u32[]{:S(2)}, u32[]{:S(2)}) %collective-permute-start.5) | collective-permute-done | bytes 294944 | tf_op jit(solution)/shard_map/ppermute | solution.py:387
  47.4 2.6 %collective-permute-done.6 = bf16[144,1024]{1,0:T(8,128)(2,1)S(1)} collective-permute-done((bf16[144,1024]{1,0:T(8,128)(2,1)S(1)}, bf16[144,1024]{1,0:T(8,128)(2,1)S(1)}, u32[]{:S(2)}, u32[]{:S(2)}) %collective-permute-start.6) | collective-permute-done | bytes 294944 | tf_op jit(solution)/shard_map/ppermute | solution.py:387
  50.8 7.8 %all-to-all-done = bf16[32,24,1024]{2,1,0:T(8,128)(2,1)} async-done(((bf16[32,24,1024]{2,1,0:T(8,128)(2,1)}), bf16[32,24,1024]{2,1,0:T(8,128)(2,1)}, u32[]{:S(2)}, u32[]{:S(2)}) %all-to-all-start) | async-done | bytes 1572896 | tf_op jit(solution)/shard_map/all_to_all | solution.py:402
  58.6 12.7 %shard_map.122 = (bf16[768,1024]{1,0:T(8,128)(2,1)}, f32[704,768]{1,0:T(8,128)}, f32[704,768]{1,0:T(8,128)}, bf16[1280,512]{1,0:T(8,128)(2,1)S(1)}) custom-call(bf16[768,1024]{1,0:T(8,128)(2,1)} %bitcast.6.recv, bf16[704,1024]{1,0:T(8,128)(2,1)S(1)} %bitcast.47, bf16[704,1024]{1,0:T(8,128)(2,1)S(1)} %bitcast.48, bf16[704,1024]{1,0:T(8,128)(2,1)} %bitcast.42, ...), custom_call_target="tpu_custom_call" | custom-call | flops 6945767424 | bytes 17825792 | tf_op jit(solution)/shard_map/pallas_call | solution.py:26
  71.3 41.7 %all_to_all.15 = bf16[32,40,512]{2,1,0:T(8,128)(2,1)S(1)} all-to-all(bf16[32,40,512]{2,1,0:T(8,128)(2,1)S(1)} %bitcast.44), channel_id=1, replica_groups=mesh['x'=4,'core'=2,'zq'=4,'zp'=2,'y'=4] {'zq','zp','y'}, dimensions={0} | all-to-all | bytes 2621440 | tf_op jit(solution)/shard_map/all_to_all | solution.py:402
  113.1 2.6 %shard_map.123 = bf16[1280,512]{1,0:T(8,128)(2,1)S(1)} custom-call(bf16[1280,512]{1,0:T(8,128)(2,1)S(1)} %bitcast.45, f32[4,128]{1,0:T(4,128)S(1)} %copy-done.8, s32[4,128]{1,0:T(4,128)S(1)} %bitcast.50, s32[4,128]{1,0:T(4,128)S(1)} %bitcast.52), custom_call_target="tpu_custom_call" | custom-call | flops 805306368 | bytes 2627584 | tf_op jit(solution)/shard_map/pallas_call | solution.py:26
  115.7 38.4 %all_to_all.16 = bf16[32,40,512]{2,1,0:T(8,128)(2,1)S(1)} all-to-all(bf16[32,40,512]{2,1,0:T(8,128)(2,1)S(1)} %bitcast.46), channel_id=1, replica_groups=mesh['x'=4,'core'=2,'zq'=4,'zp'=2,'y'=4] {'zq','zp','y'}, dimensions={0} | all-to-all | bytes 2621440 | tf_op jit(solution)/shard_map/all_to_all | solution.py:402
  154.2 4.0 %shard_map.124 = (bf16[704,768]{1,0:T(8,128)(2,1)S(1)}, bf16[704,768]{1,0:T(8,128)(2,1)S(1)}, bf16[704,768]{1,0:T(8,128)(2,1)S(1)}, bf16[768,1024]{1,0:T(8,128)(...) custom-call(bf16[1280,512]{1,0:T(8,128)(2,1)S(1)} %bitcast.41, bf16[768,1024]{1,0:T(8,128)(2,1)S(1)} %copy-done, ...), custom_call_target="tpu_custom_call" | custom-call | flops 2214592512 | bytes 14548992 | tf_op jit(solution)/shard_map/pallas_call | solution.py:26
  158.2 2.6 %shard_map.126 = (bf16[2,2112,128]{2,1,0:T(8,128)(2,1)S(1)}, bf16[2,2112,128]{2,1,0:T(8,128)(2,1)S(1)}) custom-call(bf16[704,768]{1,0:T(8,128)(2,1)S(1)} %get-tuple-element.38.d_gate, bf16[704,768]{1,0:T(8,128)(2,1)S(1)} %get-tuple-element.39.d_up, bf16[704,768]{1,0:T(8,128)(2,1)S(1)} %get-tuple-element.40.hidden, bf16[768,1024]{1,0:T(8,128)(2,1)S(1)} %copy-done, ...), custom_call_target="tpu_custom_call" | custom-call | flops 1660944384 | bytes 8552448 | tf_op jit(solution)/shard_map/pallas_call | solution.py:26
  161.4 3.0 %collective-permute-done.10.got = bf16[2112,128]{1,0:T(8,128)(2,1)S(1)} collective-permute-done((bf16[2112,128]{1,0:T(8,128)(2,1)S(1)}, bf16[2112,128]{1,0:T(8,128)(2,1)S(1)}, u32[]{:S(2)}, u32[]{:S(2)}) %collective-permute-start.10) | collective-permute-done | bytes 540704 | tf_op jit(solution)/shard_map/ppermute | solution.py:445
  166.1 1.7 collective-permute-start.12
  167.8 2.1 %shard_map.125 = (bf16[2112,128]{1,0:T(8,128)(2,1)S(1)}, bf16[2112,128]{1,0:T(8,128)(2,1)S(1)}) custom-call(bf16[704,768]{1,0:T(8,128)(2,1)S(1)} %get-tuple-element.38.d_gate, bf16[704,768]{1,0:T(8,128)(2,1)S(1)} %get-tuple-element.39.d_up, bf16[704,768]{1,0:T(8,128)(2,1)S(1)} %get-tuple-element.40.hidden, bf16[768,1024]{1,0:T(8,128)(2,1)S(1)} %copy-done, ...), custom_call_target="tpu_custom_call" | custom-call | flops 830472192 | bytes 7471104 | tf_op jit(solution)/shard_map/pallas_call | solution.py:26
  170.3 4.0 %collective-permute-done.11.b = bf16[1056,128]{1,0:T(8,128)(2,1)S(1)} collective-permute-done((bf16[1056,128]{1,0:T(8,128)(2,1)S(1)}, bf16[1056,128]{1,0:T(8,128)(2,1)S(1)}, u32[]{:S(2)}, u32[]{:S(2)}) %collective-permute-start.11) | collective-permute-done | bytes 270368 | tf_op jit(solution)/shard_map/ppermute | solution.py:454
  176.0 1.8 collective-permute-start.16
  178.0 3.0 %collective-permute-start.15 = (bf16[1056,128]{1,0:T(8,128)(2,1)S(1)}, bf16[1056,128]{1,0:T(8,128)(2,1)S(1)}, u32[]{:S(2)}, u32[]{:S(2)}) collective-permute-start(bf16[1056,128]{1,0:T(8,128)(2,1)S(1)} %get-tuple-element.54), channel_id=1, source_target_pairs={{0,192},{64,0},{128,64},{192,128},{1,193},{65,1},{129,65},{193,129... | collective-permute-start | bytes 811016 | tf_op jit(solution)/shard_map/ppermute | solution.py:458
  181.0 4.1 %collective-permute-done.13.up_late = bf16[1056,128]{1,0:T(8,128)(2,1)S(1)} collective-permute-done((bf16[1056,128]{1,0:T(8,128)(2,1)S(1)}, bf16[1056,128]{1,0:T(8,128)(2,1)S(1)}, u32[]{:S(2)}, u32[]{:S(2)}) %collective-permute-start.13) | collective-permute-done | bytes 270368 | tf_op jit(solution)/shard_map/ppermute | solution.py:464
  185.4 3.8 %collective-permute-done.14.up_now = bf16[1056,128]{1,0:T(8,128)(2,1)S(1)} collective-permute-done((bf16[1056,128]{1,0:T(8,128)(2,1)S(1)}, bf16[1056,128]{1,0:T(8,128)(2,1)S(1)}, u32[]{:S(2)}, u32[]{:S(2)}) %collective-permute-start.14) | collective-permute-done | bytes 270368 | tf_op jit(solution)/shard_map/ppermute | solution.py:457
  (50 shorter events, 16.0 us)
Async XLA Ops:
  5.1 16.8 %collective-permute-start = (bf16[144,1024]{1,0:T(8,128)(2,1)}, bf16[144,1024]{1,0:T(8,128)(2,1)S(1)}, u32[]{:S(2)}, u32[]{:S(2)}) collective-permute-start(bf16[144,1024]{1,0:T(8,128)(2,1)} %get-tuple-element.32), channel_id=1, source_target_pairs={{0,4},{4,0},{1,5},{5,1},{2,6},{6,2},{3,7},{7,3},{8,12},{12,8},{9,1... | collective-permute-start | bytes 884744 | tf_op jit(solution)/shard_map/ppermute | solution.py:387
  7.1 16.8 %collective-permute-start.1 = (bf16[144,1024]{1,0:T(8,128)(2,1)}, bf16[144,1024]{1,0:T(8,128)(2,1)S(1)}, u32[]{:S(2)}, u32[]{:S(2)}) collective-permute-start(bf16[144,1024]{1,0:T(8,128)(2,1)} %get-tuple-element.32), channel_id=1, source_target_pairs={{0,1},{1,2},{2,3},{3,0},{4,5},{5,6},{6,7},{7,4},{8,9},{9,10},{10,1... | collective-permute-start | bytes 884744 | tf_op jit(solution)/shard_map/ppermute | solution.py:387
  8.7 18.2 %collective-permute-start.2 = (bf16[144,1024]{1,0:T(8,128)(2,1)}, bf16[144,1024]{1,0:T(8,128)(2,1)}, u32[]{:S(2)}, u32[]{:S(2)}) collective-permute-start(bf16[144,1024]{1,0:T(8,128)(2,1)} %get-tuple-element.32), channel_id=1, source_target_pairs={{0,3},{1,0},{2,1},{3,2},{4,7},{5,4},{6,5},{7,6},{8,11},{9,8},{10,9... | collective-permute-start | bytes 884744 | tf_op jit(solution)/shard_map/ppermute | solution.py:387
  9.2 49.4 %all-to-all-start = ((bf16[32,24,1024]{2,1,0:T(8,128)(2,1)}), bf16[32,24,1024]{2,1,0:T(8,128)(2,1)}, u32[]{:S(2)}, u32[]{:S(2)}) async-start(bf16[32,24,1024]{2,1,0:T(8,128)(2,1)} %bitcast.53), calls=%async_computation | async-start | bytes 3145728 | tf_op jit(solution)/shard_map/all_to_all | solution.py:402
  21.9 14.4 %collective-permute-start.4 = (bf16[144,1024]{1,0:T(8,128)(2,1)S(1)}, bf16[144,1024]{1,0:T(8,128)(2,1)S(1)}, u32[]{:S(2)}, u32[]{:S(2)}) collective-permute-start(bf16[144,1024]{1,0:T(8,128)(2,1)S(1)} %collective-permute-done), channel_id=1, source_target_pairs={{0,3},{1,0},{2,1},{3,2},{4,7},{5,4},{6,5},{7,6},{8,11},{9,8},{10,9... | collective-permute-start | bytes 884744 | tf_op jit(solution)/shard_map/ppermute | solution.py:387
  22.2 16.1 %collective-permute-start.3 = (bf16[144,1024]{1,0:T(8,128)(2,1)S(1)}, bf16[144,1024]{1,0:T(8,128)(2,1)S(1)}, u32[]{:S(2)}, u32[]{:S(2)}) collective-permute-start(bf16[144,1024]{1,0:T(8,128)(2,1)S(1)} %collective-permute-done), channel_id=1, source_target_pairs={{0,1},{1,2},{2,3},{3,0},{4,5},{5,6},{6,7},{7,4},{8,9},{9,10},{10,1... | collective-permute-start | bytes 884744 | tf_op jit(solution)/shard_map/ppermute | solution.py:387
  24.0 22.7 %collective-permute-start.5 = (bf16[144,1024]{1,0:T(8,128)(2,1)S(1)}, bf16[144,1024]{1,0:T(8,128)(2,1)S(1)}, u32[]{:S(2)}, u32[]{:S(2)}) collective-permute-start(bf16[144,1024]{1,0:T(8,128)(2,1)S(1)} %collective-permute-done.1), channel_id=1, source_target_pairs={{0,1},{1,2},{2,3},{3,0},{4,5},{5,6},{6,7},{7,4},{8,9},{9,10},{10,1... | collective-permute-start | bytes 884744 | tf_op jit(solution)/shard_map/ppermute | solution.py:387
  36.3 13.7 %collective-permute-start.6 = (bf16[144,1024]{1,0:T(8,128)(2,1)S(1)}, bf16[144,1024]{1,0:T(8,128)(2,1)S(1)}, u32[]{:S(2)}, u32[]{:S(2)}) collective-permute-start(bf16[144,1024]{1,0:T(8,128)(2,1)S(1)} %collective-permute-done.4), channel_id=1, source_target_pairs={{0,3},{1,0},{2,1},{3,2},{4,7},{5,4},{6,5},{7,6},{8,11},{9,8},{10,9... | collective-permute-start | bytes 884744 | tf_op jit(solution)/shard_map/ppermute | solution.py:387
  50.8 7.8 %collective-permute-start.7 = (bf16[8,144,1024]{2,1,0:T(8,128)(2,1)}, bf16[8,144,1024]{2,1,0:T(8,128)(2,1)}, u32[]{:S(2)}, u32[]{:S(2)}) collective-permute-start(bf16[8,144,1024]{2,1,0:T(8,128)(2,1)} %bitcast_dynamic-update-slice_fusion.own_h), channel_id=1, source_target_pairs={{0,32},{32,0},{1,33},{33,1},{2,34},{34,2},{3,35},{35,3},{4,36},{36... | collective-permute-start | bytes 7077896 | tf_op jit(solution)/shard_map/ppermute | solution.py:409
  71.3 41.8 %copy-start.6 = (s32[128,4]{0,1:T(4,128)S(1)}, s32[128,4]{0,1:T(4,128)}, u32[]{:S(2)}) copy-start(s32[128,4]{0,1:T(4,128)} %param.12) | copy-start | bytes 6148
  71.3 41.8 %copy-start.7 = (s32[128,4]{0,1:T(4,128)S(1)}, s32[128,4]{0,1:T(4,128)}, u32[]{:S(2)}) copy-start(s32[128,4]{0,1:T(4,128)} %param.13) | copy-start | bytes 6148
  71.3 41.8 %copy-start.8 = (f32[4,128]{1,0:T(4,128)S(1)}, f32[4,128]{1,0:T(4,128)}, u32[]{:S(2)}) copy-start(f32[4,128]{1,0:T(4,128)} %get-tuple-element.34.weights) | copy-start | bytes 6148
  71.3 82.9 %copy-start.2 = (f32[704,768]{1,0:T(8,128)S(1)}, f32[704,768]{1,0:T(8,128)}, u32[]{:S(2)}) copy-start(f32[704,768]{1,0:T(8,128)} %get-tuple-element.37.pre_up) | copy-start | bytes 6488068
  113.1 41.1 %copy-start = (bf16[768,1024]{1,0:T(8,128)(2,1)S(1)}, bf16[768,1024]{1,0:T(8,128)(2,1)}, u32[]{:S(2)}) copy-start(bf16[768,1024]{1,0:T(8,128)(2,1)} %get-tuple-element.35.rows) | copy-start | bytes 4718596
  113.1 41.1 %copy-start.1 = (f32[704,768]{1,0:T(8,128)S(1)}, f32[704,768]{1,0:T(8,128)}, u32[]{:S(2)}) copy-start(f32[704,768]{1,0:T(8,128)} %get-tuple-element.36.pre_gate) | copy-start | bytes 6488068
  160.8 9.2 %collective-permute-start.9 = (bf16[2,2112,128]{2,1,0:T(8,128)(2,1)S(1)}, bf16[2,2112,128]{2,1,0:T(8,128)(2,1)S(1)}, u32[]{:S(2)}, u32[]{:S(2)}) collective-permute-start(bf16[2,2112,128]{2,1,0:T(8,128)(2,1)S(1)} %get-tuple-element.45), channel_id=1, source_target_pairs={{0,32},{32,0},{1,33},{33,1},{2,34},{34,2},{3,35},{35,3},{4,36},{36... | collective-permute-start | bytes 3244040 | tf_op jit(solution)/shard_map/ppermute | solution.py:448
  160.9 3.5 %collective-permute-start.10 = (bf16[2112,128]{1,0:T(8,128)(2,1)S(1)}, bf16[2112,128]{1,0:T(8,128)(2,1)S(1)}, u32[]{:S(2)}, u32[]{:S(2)}) collective-permute-start(bf16[2112,128]{1,0:T(8,128)(2,1)S(1)} %get-tuple-element.48), channel_id=1, source_target_pairs={{0,32},{32,0},{1,33},{33,1},{2,34},{34,2},{3,35},{35,3},{4,36},{36... | collective-permute-start | bytes 1622024 | tf_op jit(solution)/shard_map/ppermute | solution.py:445
  164.5 9.8 %collective-permute-start.11 = (bf16[1056,128]{1,0:T(8,128)(2,1)S(1)}, bf16[1056,128]{1,0:T(8,128)(2,1)S(1)}, u32[]{:S(2)}, u32[]{:S(2)}) collective-permute-start(bf16[1056,128]{1,0:T(8,128)(2,1)S(1)} %get-tuple-element.49), channel_id=1, source_target_pairs={{0,64},{64,128},{128,192},{192,0},{1,65},{65,129},{129,193},{193,1... | collective-permute-start | bytes 811016 | tf_op jit(solution)/shard_map/ppermute | solution.py:454
  166.1 8.2 %collective-permute-start.12 = (bf16[1056,128]{1,0:T(8,128)(2,1)S(1)}, bf16[1056,128]{1,0:T(8,128)(2,1)S(1)}, u32[]{:S(2)}, u32[]{:S(2)}) collective-permute-start(bf16[1056,128]{1,0:T(8,128)(2,1)S(1)} %get-tuple-element.51), channel_id=1, source_target_pairs={{0,192},{64,0},{128,64},{192,128},{1,193},{65,1},{129,65},{193,129... | collective-permute-start | bytes 811016 | tf_op jit(solution)/shard_map/ppermute | solution.py:455
  169.9 11.1 %collective-permute-start.8 = (bf16[2112,128]{1,0:T(8,128)(2,1)S(1)}, bf16[2112,128]{1,0:T(8,128)(2,1)S(1)}, u32[]{:S(2)}, u32[]{:S(2)}) collective-permute-start(bf16[2112,128]{1,0:T(8,128)(2,1)S(1)} %get-tuple-element.43), channel_id=1, source_target_pairs={{0,32},{32,0},{1,33},{33,1},{2,34},{34,2},{3,35},{35,3},{4,36},{36... | collective-permute-start | bytes 1622024 | tf_op jit(solution)/shard_map/ppermute | solution.py:462
  174.5 10.6 %collective-permute-start.13 = (bf16[1056,128]{1,0:T(8,128)(2,1)S(1)}, bf16[1056,128]{1,0:T(8,128)(2,1)S(1)}, u32[]{:S(2)}, u32[]{:S(2)}) collective-permute-start(bf16[1056,128]{1,0:T(8,128)(2,1)S(1)} %get-tuple-element.52), channel_id=1, source_target_pairs={{0,64},{64,128},{128,192},{192,0},{1,65},{65,129},{129,193},{193,1... | collective-permute-start | bytes 811016 | tf_op jit(solution)/shard_map/ppermute | solution.py:464
  176.0 9.4 %collective-permute-start.16 = (bf16[1056,128]{1,0:T(8,128)(2,1)S(1)}, bf16[1056,128]{1,0:T(8,128)(2,1)S(1)}, u32[]{:S(2)}, u32[]{:S(2)}) collective-permute-start(bf16[1056,128]{1,0:T(8,128)(2,1)S(1)} %get-tuple-element.55), channel_id=1, source_target_pairs={{0,192},{64,0},{128,64},{192,128},{1,193},{65,1},{129,65},{193,129... | collective-permute-start | bytes 811016 | tf_op jit(solution)/shard_map/ppermute | solution.py:465
  177.8 11.4 %collective-permute-start.14 = (bf16[1056,128]{1,0:T(8,128)(2,1)S(1)}, bf16[1056,128]{1,0:T(8,128)(2,1)S(1)}, u32[]{:S(2)}, u32[]{:S(2)}) collective-permute-start(bf16[1056,128]{1,0:T(8,128)(2,1)S(1)} %get-tuple-element.53), channel_id=1, source_target_pairs={{0,64},{64,128},{128,192},{192,0},{1,65},{65,129},{129,193},{193,1... | collective-permute-start | bytes 811016 | tf_op jit(solution)/shard_map/ppermute | solution.py:457
  178.0 11.2 %collective-permute-start.15 = (bf16[1056,128]{1,0:T(8,128)(2,1)S(1)}, bf16[1056,128]{1,0:T(8,128)(2,1)S(1)}, u32[]{:S(2)}, u32[]{:S(2)}) collective-permute-start(bf16[1056,128]{1,0:T(8,128)(2,1)S(1)} %get-tuple-element.54), channel_id=1, source_target_pairs={{0,192},{64,0},{128,64},{192,128},{1,193},{65,1},{129,65},{193,129... | collective-permute-start | bytes 811016 | tf_op jit(solution)/shard_map/ppermute | solution.py:458
  (3 other events, 118.2 us)
where the time goes:
time: 192 us; the launch traced here: 190 us
  blocking collectives  80.2 us (42%)
  waiting for transfers between devices  40.3 us (21%)
  starting transfers between devices  30.9 us (16%)
  Pallas kernels  30.2 us (16%)
  local copies, waits for them, and re-layouts  8.04 us (4%)
    all_to_all x2, blocking collectives, exchange(): out = lax.all_to_all(v, EXPERT, 0, 0, tiled=True)  80.2 us
    pallas_call x10, Pallas kernels, call(): pl.pallas_call(body, out_shape=tuple(outs), in_specs=specs or [VMEM] * le...  30.2 us
    ppermute x7, waiting for transfers between devices, shift(): return lax.ppermute(v, axis, [(s, (s + by) % size) for s in range(size)])  17.3 us
    all_to_all x1, starting transfers between devices, exchange(): out = lax.all_to_all(v, EXPERT, 0, 0, tiled=True)  10.8 us
    ppermute x7, starting transfers between devices, shift(): return lax.ppermute(v, axis, [(s, (s + by) % size) for s in range(size)])  9.46 us
    all_to_all x1, waiting for transfers between devices, exchange(): out = lax.all_to_all(v, EXPERT, 0, 0, tiled=True)  7.76 us
    unnamed x25, local copies, waits for them, and re-layouts  7.28 us
    ppermute x1, waiting for transfers between devices, on_device(): late_up = lax.ppermute(late_up, 'x', up)  4.09 us
  transfers between devices with their start and end apart: 18, of which 9 were waited for; matrix products, arithmetic and copies ran while one was open for 4% of the time, Pallas kernels for 1%

commit v1 on v0

--- a/solution.py
+++ b/solution.py
@@ -157,10 +157,14 @@
 
 
 def forward_body(
-    cap, recv, gate, up, down_h, own_h, other_h, rows, pre_gate, pre_up, ret,
-    down, own, other, x_out, g_out, u_out, sems,
+    cap, recv, gate, up, down_h, own_h, own_far_h, other_h, other_far_h, rows, slope, act, middle,
+    ret, down, piece, x_out, slope_out, act_out, middle_out, sems,
 ):
-    copies = fetch([(down_h, down), (own_h, own), (other_h, other)], sems)
+    pairs, first_unit = [(down_h, down)], 0
+    for source in (own_h, own_far_h, other_h, other_far_h):
+        pairs.append((source, piece.at[first_unit : first_unit + source.shape[0]]))
+        first_unit += source.shape[0]
+    copies = fetch(pairs, sems)
     count, model = recv.shape
 
     def save(src, dst, at):
@@ -174,7 +178,7 @@
     keep = as_bf16(slot < cap)
     x = recv[...] * jnp.concatenate([keep] * (model // 128), axis=1)
     x_out[...] = x
-    saves = [save(x_out, rows, 3)]
+    saves = [save(x_out, rows, 5)]
     pick = as_bf16(iota((experts, count), 1) == iota((experts, count), 0) * STEP + cap)
     found = nn(pick, recv[:, 0:256]).astype(BF16)
     row = iota((count, experts), 0)
@@ -185,22 +189,26 @@
     mine = jnp.logical_and(iota((count, 128), 1) == slot, slot < cap)
     weight = jnp.sum(jnp.where(mine, wide, 0.0), axis=1, keepdims=True)
     g = nt(gate[...], x)
-    g_out[...] = g
-    saves.append(save(g_out, pre_gate, 4))
     u = nt(up[...], x)
-    u_out[...] = u
-    saves.append(save(u_out, pre_up, 5))
-    hidden = (g * sigmoid(g) * u).astype(BF16)
+    s = sigmoid(g)
+    a = g * s
+    act_out[...] = a
+    saves.append(save(act_out, act, 6))
+    slope_out[...] = u * s * (1.0 + g * (1.0 - s))
+    saves.append(save(slope_out, slope, 7))
+    hidden = (a * u).astype(BF16)
+    middle_out[...] = hidden
+    saves.append(save(middle_out, middle, 8))
     copies[0].wait()
     acc = weight * tn(hidden, down[...])
-    for copy, piece in zip(copies[1:], (own, other)):
-        units = piece.shape[1] // 3
-        take = lambda i: piece[:, i * units : (i + 1) * units, :].reshape(-1, model)
+    units = piece.shape[1] // 3
+    take = lambda i: piece[:, i * units : (i + 1) * units, :].reshape(-1, model)
+    for copy in copies[1:]:
         copy.wait()
-        a = nt(take(0), x)
-        b = nt(take(1), x)
-        hidden = (a * sigmoid(a) * b).astype(BF16)
-        acc = acc - tn(hidden, take(2))
+    a = nt(take(0), x)
+    b = nt(take(1), x)
+    hidden = (a * sigmoid(a) * b).astype(BF16)
+    acc = acc - tn(hidden, take(2))
     result = acc.astype(BF16)
     pack = packing(cap, False)
     tall = 4 * STEP
@@ -286,7 +294,7 @@
     return put
 
 
-def grad_body(cap, wire, rows, pre_gate, pre_up, down, d_gate, d_up, hidden, cot, mine, theirs):
+def grad_body(cap, wire, rows, slope, act, hidden, down, d_gate, d_up, cot, mine, theirs):
     count, model = cot.shape
     unpack = packing(cap, True)
     tall = 4 * STEP
@@ -295,17 +303,9 @@
         cot[i * tall : (i + 1) * tall, : model // 2] = both[:tall]
         cot[i * tall : (i + 1) * tall, model // 2 :] = both[tall:]
     grad_hidden = nt(down[...], cot[...])
-    g = pre_gate[...]
-    u = pre_up[...]
-    s = sigmoid(g)
-    act = g * s
-    parts = (
-        (grad_hidden * u * s * (1.0 + g * (1.0 - s))).astype(BF16),
-        (grad_hidden * act).astype(BF16),
-        (act * u).astype(BF16),
-    )
-    for ref, value in zip((d_gate, d_up, hidden), parts):
-        ref[...] = value
+    d_gate[...] = (grad_hidden * slope[...]).astype(BF16)
+    d_up[...] = (grad_hidden * act[...]).astype(BF16)
+    parts = (d_gate[...], d_up[...], hidden[...])
     chunk(parts, rows, cot, (2,), [(putter(mine), putter(theirs))])
 
 
@@ -393,9 +393,8 @@
     pair_before = shift(pair, "y", 4, -1)
     far = shift(after, "y", 4, 1)
     pair_far = shift(pair_before, "y", 4, -1)
-    gathered = jnp.stack(
-        [shard, pair, after, before, pair_after, pair_before, far, pair_far], axis=0
-    )
+    gathered = jnp.stack([shard, pair, after, before, pair_after, pair_before], axis=0)
+    gathered_far = jnp.stack([far, pair_far], axis=0)
 
     def exchange(v):
         v = v.reshape(experts, -1, v.shape[1])
@@ -407,19 +406,23 @@
     weight_buf = pltpu.VMEM((width, model), BF16)
     swap = [(0, 1), (1, 0)]
     other = lax.ppermute(gathered, "core", swap)
-    piece_buf = pltpu.VMEM(gathered.shape, BF16)
-    x, pre_gate, pre_up, ret = call(
+    other_far = lax.ppermute(gathered_far, "core", swap)
+    x, slope, act, hidden, ret = call(
         functools.partial(forward_body, cap),
         [shape((rows, model), BF16), shape((width, rows), F32), shape((width, rows), F32)]
-        + [shape((2 * experts * cap, model // 2), BF16)],
-        [recv, gate_t, up_t, down, gathered, other],
-        specs=[VMEM] * 3 + [HBM] * 3,
-        out_specs=[HBM, HBM, HBM, VMEM],
-        scratch=[weight_buf]
-        + [piece_buf] * 2
-        + [pltpu.VMEM((rows, model), BF16)]
-        + [pltpu.VMEM((width, rows), F32)] * 2
-        + [pltpu.SemaphoreType.DMA((6,))],
+        + [shape((width, rows), BF16), shape((2 * experts * cap, model // 2), BF16)],
+        [recv, gate_t, up_t, down, gathered, gathered_far, other, other_far],
+        specs=[VMEM] * 3 + [HBM] * 5,
+        out_specs=[HBM, HBM, HBM, HBM, VMEM],
+        scratch=[
+            weight_buf,
+            pltpu.VMEM((16,) + shard.shape, BF16),
+            pltpu.VMEM((rows, model), BF16),
+            pltpu.VMEM((width, rows), F32),
+            pltpu.VMEM((width, rows), F32),
+            pltpu.VMEM((width, rows), BF16),
+            pltpu.SemaphoreType.DMA((9,)),
+        ],
         flops=6 * rows * (width + 768) * model,
         grant=GRANT_F,
     )
@@ -435,10 +438,10 @@
     tall = 3 * width
     side = shape((width, rows), BF16)
     one, two = shape((tall, 128), BF16), shape((2, tall, 128), BF16)
-    d_gate, d_up, hidden, cot, far_mine, far_theirs = call(
+    d_gate, d_up, cot, far_mine, far_theirs = call(
         functools.partial(grad_body, cap),
-        [side] * 3 + [shape((rows, model), BF16)] + [one] * 2,
-        [exchange(cot_send), x, pre_gate, pre_up, down],
+        [side] * 2 + [shape((rows, model), BF16)] + [one] * 2,
+        [exchange(cot_send), x, slope, act, hidden, down],
         flops=4 * rows * width * model,
         grant=GRANT_G,
     )

time: 192 us -> 190 us (0.990)
  waiting for transfers between devices: 40.3 us -> 48.2 us
  local copies, waits for them, and re-layouts: 8.04 us -> 0.18 us
  Pallas kernels: 30.2 us -> 28 us
    ppermute x7, waiting for transfers between devices: 17.3 us -> 27.8 us  [shift(): return lax.ppermute(v, axis, [(s, (s + by) % size) for s in range(size)])]
    unnamed x25, local copies, waits for them, and re-layouts: 7.28 us -> 0.16 us
    all_to_all x1, waiting for transfers between devices: 7.76 us -> 3.19 us  [exchange(): out = lax.all_to_all(v, EXPERT, 0, 0, tiled=True)]
    pallas_call x10, Pallas kernels: 30.2 us -> 28 us  [call(): pl.pallas_call(body, out_shape=tuple(outs), in_specs=specs or [VMEM] * le...]
    ppermute x0 -> x1, waiting for transfers between devices: none -> 1.99 us  [on_device(): other_far = lax.ppermute(gathered_far, 'core', swap)]
  transfers between devices with their start and end apart: 18 -> 19, of which waited for: 9 -> 10; matrix products, arithmetic and copies ran while one was open for 4% -> 0% of each run, Pallas kernels for 1% -> 1%
where the time goes in v1:
time: 190 us; the launch traced here: 188 us
  blocking collectives  78.9 us (42%)
  waiting for transfers between devices  48.2 us (25%)
  starting transfers between devices  31.7 us (17%)
  Pallas kernels  28 us (15%)
    all_to_all x2, blocking collectives, exchange(): out = lax.all_to_all(v, EXPERT, 0, 0, tiled=True)  78.9 us
    pallas_call x10, Pallas kernels, call(): pl.pallas_call(body, out_shape=tuple(outs), in_specs=specs or [VMEM] * le...  28 us
    ppermute x7, waiting for transfers between devices, shift(): return lax.ppermute(v, axis, [(s, (s + by) % size) for s in range(size)])  27.8 us
    all_to_all x1, starting transfers between devices, exchange(): out = lax.all_to_all(v, EXPERT, 0, 0, tiled=True)  11.9 us
    ppermute x7, starting transfers between devices, shift(): return lax.ppermute(v, axis, [(s, (s + by) % size) for s in range(size)])  8.87 us
    ppermute x1, waiting for transfers between devices, on_device(): late_up = lax.ppermute(late_up, 'x', up)  4.08 us
    ppermute x1, waiting for transfers between devices, on_device(): a = lax.ppermute(far_up, 'x', up)  4.02 us
    ppermute x1, waiting for transfers between devices, on_device(): now_up = lax.ppermute(up_now, 'x', up)  3.85 us
  transfers between devices with their start and end apart: 19, of which 10 were waited for; matrix products, arithmetic and copies ran while one was open for 0% of the time, Pallas kernels for 1%

profile of v1, /device:TPU:8, one launch (start us, length us, event | category | flops | bytes accessed | tf_op | source)
XLA Modules:
  0.0 188.0 jit_solution(18189869136021391659)
XLA Ops:
  0.6 4.5 %shard_map.121 = (bf16[768,1024]{1,0:T(8,128)(2,1)}, f32[4,128]{1,0:T(4,128)}, bf16[144,1024]{1,0:T(8,128)(2,1)}) custom-call(bf16[128,1024]{1,0:T(8,128)(2,1)} %tok_h.1, f32[32,1024]{1,0:T(8,128)} %bitcast.59, s32[4,128]{1,0:T(4,128)} %bitcast.46, s32[4,128]{1,0:T(4,128)} %bitcast.48, bf16[86,1024]{1,0:T(8,128)(2,1)} %bitcast.57, ...), custom_call_target="tpu_custom_call" | custom-call | flops 402653184 | bytes 2795520 | tf_op jit(solution)/shard_map/pallas_call | solution.py:26
  5.2 2.0 %collective-permute-start = (bf16[144,1024]{1,0:T(8,128)(2,1)}, bf16[144,1024]{1,0:T(8,128)(2,1)S(1)}, u32[]{:S(2)}, u32[]{:S(2)}) collective-permute-start(bf16[144,1024]{1,0:T(8,128)(2,1)} %get-tuple-element.32), channel_id=1, source_target_pairs={{0,4},{4,0},{1,5},{5,1},{2,6},{6,2},{3,7},{7,3},{8,12},{12,8},{9,1... | collective-permute-start | bytes 884744 | tf_op jit(solution)/shard_map/ppermute | solution.py:387
  7.6 1.6 collective-permute-start.1
  9.2 11.9 %all-to-all-start = ((bf16[32,24,1024]{2,1,0:T(8,128)(2,1)}), bf16[32,24,1024]{2,1,0:T(8,128)(2,1)}, u32[]{:S(2)}, u32[]{:S(2)}) async-start(bf16[32,24,1024]{2,1,0:T(8,128)(2,1)} %bitcast.50), calls=%async_computation | async-start | bytes 3145728 | tf_op jit(solution)/shard_map/all_to_all | solution.py:401
  21.5 1.7 collective-permute-start.3
  23.3 12.8 %collective-permute-done.3 = bf16[144,1024]{1,0:T(8,128)(2,1)S(1)} collective-permute-done((bf16[144,1024]{1,0:T(8,128)(2,1)S(1)}, bf16[144,1024]{1,0:T(8,128)(2,1)S(1)}, u32[]{:S(2)}, u32[]{:S(2)}) %collective-permute-start.3) | collective-permute-done | bytes 294944 | tf_op jit(solution)/shard_map/ppermute | solution.py:387
  39.1 13.0 %collective-permute-done.5 = bf16[144,1024]{1,0:T(8,128)(2,1)S(1)} collective-permute-done((bf16[144,1024]{1,0:T(8,128)(2,1)S(1)}, bf16[144,1024]{1,0:T(8,128)(2,1)S(1)}, u32[]{:S(2)}, u32[]{:S(2)}) %collective-permute-start.5) | collective-permute-done | bytes 294944 | tf_op jit(solution)/shard_map/ppermute | solution.py:387
  52.1 2.0 %collective-permute-done.6 = bf16[144,1024]{1,0:T(8,128)(2,1)S(1)} collective-permute-done((bf16[144,1024]{1,0:T(8,128)(2,1)S(1)}, bf16[144,1024]{1,0:T(8,128)(2,1)S(1)}, u32[]{:S(2)}, u32[]{:S(2)}) %collective-permute-start.6) | collective-permute-done | bytes 294944 | tf_op jit(solution)/shard_map/ppermute | solution.py:387
  54.4 2.0 %collective-permute-done.8.other_far_h = bf16[2,144,1024]{2,1,0:T(8,128)(2,1)S(1)} collective-permute-done((bf16[2,144,1024]{2,1,0:T(8,128)(2,1)S(1)}, bf16[2,144,1024]{2,1,0:T(8,128)(2,1)S(1)}, u32[]{:S(2)}, u32[]{:S(2)}) %collective-permute-start.8) | collective-permute-done | bytes 589856 | tf_op jit(solution)/shard_map/ppermute | solution.py:409
  56.4 3.2 %all-to-all-done = bf16[32,24,1024]{2,1,0:T(8,128)(2,1)} async-done(((bf16[32,24,1024]{2,1,0:T(8,128)(2,1)}), bf16[32,24,1024]{2,1,0:T(8,128)(2,1)}, u32[]{:S(2)}, u32[]{:S(2)}) %all-to-all-start) | async-done | bytes 1572896 | tf_op jit(solution)/shard_map/all_to_all | solution.py:401
  59.6 10.8 %shard_map.122 = (bf16[768,1024]{1,0:T(8,128)(2,1)}, f32[704,768]{1,0:T(8,128)}, f32[704,768]{1,0:T(8,128)}, bf16[704,768]{1,0:T(8,128)(2,1)S(1)}, bf16[1280,512]{1,0:T(8,128)(2,1)S(1)}) custom-call(bf16[768,1024]{1,0:T(8,128)(2,1)} %bitcast.6.recv, bf16[704,1024]{1,0:T(8,128)(2,1)S(1)} %bitcast.45, bf16[704,1024]{1,0:T(8,128)(2,1)} %bitcast.53, ...), custom_call_target="tpu_custom_call" | custom-call | flops 6945767424 | bytes 18907136 | tf_op jit(solution)/shard_map/pallas_call | solution.py:26
  70.5 40.3 %all_to_all.15 = bf16[32,40,512]{2,1,0:T(8,128)(2,1)S(1)} all-to-all(bf16[32,40,512]{2,1,0:T(8,128)(2,1)S(1)} %bitcast.42), channel_id=1, replica_groups=mesh['x'=4,'core'=2,'zq'=4,'zp'=2,'y'=4] {'zq','zp','y'}, dimensions={0} | all-to-all | bytes 2621440 | tf_op jit(solution)/shard_map/all_to_all | solution.py:401
  110.8 2.7 %shard_map.123 = bf16[1280,512]{1,0:T(8,128)(2,1)S(1)} custom-call(bf16[1280,512]{1,0:T(8,128)(2,1)S(1)} %bitcast.43, f32[4,128]{1,0:T(4,128)S(1)} %copy-done.7, s32[4,128]{1,0:T(4,128)S(1)} %bitcast.47, s32[4,128]{1,0:T(4,128)S(1)} %bitcast.49), custom_call_target="tpu_custom_call" | custom-call | flops 805306368 | bytes 2627584 | tf_op jit(solution)/shard_map/pallas_call | solution.py:26
  113.5 38.6 %all_to_all.16 = bf16[32,40,512]{2,1,0:T(8,128)(2,1)S(1)} all-to-all(bf16[32,40,512]{2,1,0:T(8,128)(2,1)S(1)} %bitcast.44), channel_id=1, replica_groups=mesh['x'=4,'core'=2,'zq'=4,'zp'=2,'y'=4] {'zq','zp','y'}, dimensions={0} | all-to-all | bytes 2621440 | tf_op jit(solution)/shard_map/all_to_all | solution.py:401
  152.1 3.7 %shard_map.124 = (bf16[704,768]{1,0:T(8,128)(2,1)S(1)}, bf16[704,768]{1,0:T(8,128)(2,1)S(1)}, bf16[768,1024]{1,0:T(8,128)(2,1)S(1)}, bf16[2112,128]{1,0:T(8,128)(2,1)S(1)}, bf16[2112,128]{1,0:T(8,128)(2,1)S(1)}) custom-call(bf16[1280,512]{1,0:T(8,128)(2,1)S(1)} %bitcast.39, bf16[768,1024]{1,0:T(8,128)(2,1)S(1)} %copy-done, f32[704,768]{1,0:T(8,128)S(1)} %copy-done.1, ...), custom_call_target="tpu_custom_call" | custom-call | flops 2214592512 | bytes 14548992 | tf_op jit(solution)/shard_map/pallas_call | solution.py:26
  155.9 2.6 %shard_map.126 = (bf16[2,2112,128]{2,1,0:T(8,128)(2,1)S(1)}, bf16[2,2112,128]{2,1,0:T(8,128)(2,1)S(1)}) custom-call(bf16[704,768]{1,0:T(8,128)(2,1)S(1)} %get-tuple-element.39.d_gate, bf16[704,768]{1,0:T(8,128)(2,1)S(1)} %get-tuple-element.40.d_up, bf16[704,768]{1,0:T(8,128)(2,1)S(1)} %get-tuple-element.38.hidden, bf16[768,1024]{1,0:T(8,128)(2,1)S(1)} %copy-done, ...), custom_call_target="tpu_custom_call" | custom-call | flops 1660944384 | bytes 8552448 | tf_op jit(solution)/shard_map/pallas_call | solution.py:26
  159.1 3.0 %collective-permute-done.11.got = bf16[2112,128]{1,0:T(8,128)(2,1)S(1)} collective-permute-done((bf16[2112,128]{1,0:T(8,128)(2,1)S(1)}, bf16[2112,128]{1,0:T(8,128)(2,1)S(1)}, u32[]{:S(2)}, u32[]{:S(2)}) %collective-permute-start.11) | collective-permute-done | bytes 540704 | tf_op jit(solution)/shard_map/ppermute | solution.py:448
  163.7 1.8 collective-permute-start.13
  165.5 2.1 %shard_map.125 = (bf16[2112,128]{1,0:T(8,128)(2,1)S(1)}, bf16[2112,128]{1,0:T(8,128)(2,1)S(1)}) custom-call(bf16[704,768]{1,0:T(8,128)(2,1)S(1)} %get-tuple-element.39.d_gate, bf16[704,768]{1,0:T(8,128)(2,1)S(1)} %get-tuple-element.40.d_up, bf16[704,768]{1,0:T(8,128)(2,1)S(1)} %get-tuple-element.38.hidden, bf16[768,1024]{1,0:T(8,128)(2,1)S(1)} %copy-done, ...), custom_call_target="tpu_custom_call" | custom-call | flops 830472192 | bytes 7471104 | tf_op jit(solution)/shard_map/pallas_call | solution.py:26
  167.9 4.0 %collective-permute-done.12.b = bf16[1056,128]{1,0:T(8,128)(2,1)S(1)} collective-permute-done((bf16[1056,128]{1,0:T(8,128)(2,1)S(1)}, bf16[1056,128]{1,0:T(8,128)(2,1)S(1)}, u32[]{:S(2)}, u32[]{:S(2)}) %collective-permute-start.12) | collective-permute-done | bytes 270368 | tf_op jit(solution)/shard_map/ppermute | solution.py:457
  173.6 1.8 collective-permute-start.17
  175.7 3.0 %collective-permute-start.16 = (bf16[1056,128]{1,0:T(8,128)(2,1)S(1)}, bf16[1056,128]{1,0:T(8,128)(2,1)S(1)}, u32[]{:S(2)}, u32[]{:S(2)}) collective-permute-start(bf16[1056,128]{1,0:T(8,128)(2,1)S(1)} %get-tuple-element.54), channel_id=1, source_target_pairs={{0,192},{64,0},{128,64},{192,128},{1,193},{65,1},{129,65},{193,129... | collective-permute-start | bytes 811016 | tf_op jit(solution)/shard_map/ppermute | solution.py:461
  178.6 4.1 %collective-permute-done.14.up_late = bf16[1056,128]{1,0:T(8,128)(2,1)S(1)} collective-permute-done((bf16[1056,128]{1,0:T(8,128)(2,1)S(1)}, bf16[1056,128]{1,0:T(8,128)(2,1)S(1)}, u32[]{:S(2)}, u32[]{:S(2)}) %collective-permute-start.14) | collective-permute-done | bytes 270368 | tf_op jit(solution)/shard_map/ppermute | solution.py:467
  183.0 3.8 %collective-permute-done.15.up_now = bf16[1056,128]{1,0:T(8,128)(2,1)S(1)} collective-permute-done((bf16[1056,128]{1,0:T(8,128)(2,1)S(1)}, bf16[1056,128]{1,0:T(8,128)(2,1)S(1)}, u32[]{:S(2)}, u32[]{:S(2)}) %collective-permute-start.15) | collective-permute-done | bytes 270368 | tf_op jit(solution)/shard_map/ppermute | solution.py:460
  (53 shorter events, 10.1 us)
Async XLA Ops:
  5.2 16.0 %collective-permute-start = (bf16[144,1024]{1,0:T(8,128)(2,1)}, bf16[144,1024]{1,0:T(8,128)(2,1)S(1)}, u32[]{:S(2)}, u32[]{:S(2)}) collective-permute-start(bf16[144,1024]{1,0:T(8,128)(2,1)} %get-tuple-element.32), channel_id=1, source_target_pairs={{0,4},{4,0},{1,5},{5,1},{2,6},{6,2},{3,7},{7,3},{8,12},{12,8},{9,1... | collective-permute-start | bytes 884744 | tf_op jit(solution)/shard_map/ppermute | solution.py:387
  7.2 16.1 %collective-permute-start.2 = (bf16[144,1024]{1,0:T(8,128)(2,1)}, bf16[144,1024]{1,0:T(8,128)(2,1)S(1)}, u32[]{:S(2)}, u32[]{:S(2)}) collective-permute-start(bf16[144,1024]{1,0:T(8,128)(2,1)} %get-tuple-element.32), channel_id=1, source_target_pairs={{0,3},{1,0},{2,1},{3,2},{4,7},{5,4},{6,5},{7,6},{8,11},{9,8},{10,9... | collective-permute-start | bytes 884744 | tf_op jit(solution)/shard_map/ppermute | solution.py:387
  7.6 15.7 %collective-permute-start.1 = (bf16[144,1024]{1,0:T(8,128)(2,1)}, bf16[144,1024]{1,0:T(8,128)(2,1)S(1)}, u32[]{:S(2)}, u32[]{:S(2)}) collective-permute-start(bf16[144,1024]{1,0:T(8,128)(2,1)} %get-tuple-element.32), channel_id=1, source_target_pairs={{0,1},{1,2},{2,3},{3,0},{4,5},{5,6},{6,7},{7,4},{8,9},{9,10},{10,1... | collective-permute-start | bytes 884744 | tf_op jit(solution)/shard_map/ppermute | solution.py:387
  9.2 50.4 %all-to-all-start = ((bf16[32,24,1024]{2,1,0:T(8,128)(2,1)}), bf16[32,24,1024]{2,1,0:T(8,128)(2,1)}, u32[]{:S(2)}, u32[]{:S(2)}) async-start(bf16[32,24,1024]{2,1,0:T(8,128)(2,1)} %bitcast.50), calls=%async_computation | async-start | bytes 3145728 | tf_op jit(solution)/shard_map/all_to_all | solution.py:401
  21.1 15.1 %collective-permute-start.4 = (bf16[144,1024]{1,0:T(8,128)(2,1)S(1)}, bf16[144,1024]{1,0:T(8,128)(2,1)S(1)}, u32[]{:S(2)}, u32[]{:S(2)}) collective-permute-start(bf16[144,1024]{1,0:T(8,128)(2,1)S(1)} %collective-permute-done), channel_id=1, source_target_pairs={{0,3},{1,0},{2,1},{3,2},{4,7},{5,4},{6,5},{7,6},{8,11},{9,8},{10,9... | collective-permute-start | bytes 884744 | tf_op jit(solution)/shard_map/ppermute | solution.py:387
  21.5 14.7 %collective-permute-start.3 = (bf16[144,1024]{1,0:T(8,128)(2,1)S(1)}, bf16[144,1024]{1,0:T(8,128)(2,1)S(1)}, u32[]{:S(2)}, u32[]{:S(2)}) collective-permute-start(bf16[144,1024]{1,0:T(8,128)(2,1)S(1)} %collective-permute-done), channel_id=1, source_target_pairs={{0,1},{1,2},{2,3},{3,0},{4,5},{5,6},{6,7},{7,4},{8,9},{9,10},{10,1... | collective-permute-start | bytes 884744 | tf_op jit(solution)/shard_map/ppermute | solution.py:387
  36.3 20.1 %collective-permute-start.7 = (bf16[6,144,1024]{2,1,0:T(8,128)(2,1)S(1)}, bf16[6,144,1024]{2,1,0:T(8,128)(2,1)}, u32[]{:S(2)}, u32[]{:S(2)}) collective-permute-start(bf16[6,144,1024]{2,1,0:T(8,128)(2,1)S(1)} %bitcast_dynamic-update-slice_fusion.own_h), channel_id=1, source_target_pairs={{0,32},{32,0},{1,33},{33,1},{2,34},{34,2},{3,35},{35,3},{4,36},{36... | collective-permute-start | bytes 5308424 | tf_op jit(solution)/shard_map/ppermute | solution.py:408
  36.4 15.7 %collective-permute-start.5 = (bf16[144,1024]{1,0:T(8,128)(2,1)S(1)}, bf16[144,1024]{1,0:T(8,128)(2,1)S(1)}, u32[]{:S(2)}, u32[]{:S(2)}) collective-permute-start(bf16[144,1024]{1,0:T(8,128)(2,1)S(1)} %collective-permute-done.1), channel_id=1, source_target_pairs={{0,1},{1,2},{2,3},{3,0},{4,5},{5,6},{6,7},{7,4},{8,9},{9,10},{10,1... | collective-permute-start | bytes 884744 | tf_op jit(solution)/shard_map/ppermute | solution.py:387
  37.8 16.2 %collective-permute-start.6 = (bf16[144,1024]{1,0:T(8,128)(2,1)S(1)}, bf16[144,1024]{1,0:T(8,128)(2,1)S(1)}, u32[]{:S(2)}, u32[]{:S(2)}) collective-permute-start(bf16[144,1024]{1,0:T(8,128)(2,1)S(1)} %collective-permute-done.4), channel_id=1, source_target_pairs={{0,3},{1,0},{2,1},{3,2},{4,7},{5,4},{6,5},{7,6},{8,11},{9,8},{10,9... | collective-permute-start | bytes 884744 | tf_op jit(solution)/shard_map/ppermute | solution.py:387
  54.1 2.3 %collective-permute-start.8 = (bf16[2,144,1024]{2,1,0:T(8,128)(2,1)S(1)}, bf16[2,144,1024]{2,1,0:T(8,128)(2,1)S(1)}, u32[]{:S(2)}, u32[]{:S(2)}) collective-permute-start(bf16[2,144,1024]{2,1,0:T(8,128)(2,1)S(1)} %pad_maximum_fusion.own_far_h), channel_id=1, source_target_pairs={{0,32},{32,0},{1,33},{33,1},{2,34},{34,2},{3,35},{35,3},{4,36},{36... | collective-permute-start | bytes 1769480 | tf_op jit(solution)/shard_map/ppermute | solution.py:409
  70.4 40.4 %copy-start.5 = (s32[128,4]{0,1:T(4,128)S(1)}, s32[128,4]{0,1:T(4,128)}, u32[]{:S(2)}) copy-start(s32[128,4]{0,1:T(4,128)} %param.12) | copy-start | bytes 6148
  70.4 40.4 %copy-start.6 = (s32[128,4]{0,1:T(4,128)S(1)}, s32[128,4]{0,1:T(4,128)}, u32[]{:S(2)}) copy-start(s32[128,4]{0,1:T(4,128)} %param.13) | copy-start | bytes 6148
  70.5 81.6 %copy-start.2 = (f32[704,768]{1,0:T(8,128)S(1)}, f32[704,768]{1,0:T(8,128)}, u32[]{:S(2)}) copy-start(f32[704,768]{1,0:T(8,128)} %get-tuple-element.37.act) | copy-start | bytes 6488068
  110.8 41.3 %copy-start.1 = (f32[704,768]{1,0:T(8,128)S(1)}, f32[704,768]{1,0:T(8,128)}, u32[]{:S(2)}) copy-start(f32[704,768]{1,0:T(8,128)} %get-tuple-element.36.slope) | copy-start | bytes 6488068
  110.8 41.3 %copy-start.3 = (bf16[1,704,1024]{2,1,0:T(8,128)(2,1)S(1)}, bf16[1,704,1024]{2,1,0:T(8,128)(2,1)}, u32[]{:S(2)}) copy-start(bf16[1,704,1024]{2,1,0:T(8,128)(2,1)} %param.19) | copy-start | bytes 4325380
  158.5 9.2 %collective-permute-start.10 = (bf16[2,2112,128]{2,1,0:T(8,128)(2,1)S(1)}, bf16[2,2112,128]{2,1,0:T(8,128)(2,1)S(1)}, u32[]{:S(2)}, u32[]{:S(2)}) collective-permute-start(bf16[2,2112,128]{2,1,0:T(8,128)(2,1)S(1)} %get-tuple-element.45), channel_id=1, source_target_pairs={{0,32},{32,0},{1,33},{33,1},{2,34},{34,2},{3,35},{35,3},{4,36},{36... | collective-permute-start | bytes 3244040 | tf_op jit(solution)/shard_map/ppermute | solution.py:451
  158.6 3.5 %collective-permute-start.11 = (bf16[2112,128]{1,0:T(8,128)(2,1)S(1)}, bf16[2112,128]{1,0:T(8,128)(2,1)S(1)}, u32[]{:S(2)}, u32[]{:S(2)}) collective-permute-start(bf16[2112,128]{1,0:T(8,128)(2,1)S(1)} %get-tuple-element.48), channel_id=1, source_target_pairs={{0,32},{32,0},{1,33},{33,1},{2,34},{34,2},{3,35},{35,3},{4,36},{36... | collective-permute-start | bytes 1622024 | tf_op jit(solution)/shard_map/ppermute | solution.py:448
  162.2 9.8 %collective-permute-start.12 = (bf16[1056,128]{1,0:T(8,128)(2,1)S(1)}, bf16[1056,128]{1,0:T(8,128)(2,1)S(1)}, u32[]{:S(2)}, u32[]{:S(2)}) collective-permute-start(bf16[1056,128]{1,0:T(8,128)(2,1)S(1)} %get-tuple-element.49), channel_id=1, source_target_pairs={{0,64},{64,128},{128,192},{192,0},{1,65},{65,129},{129,193},{193,1... | collective-permute-start | bytes 811016 | tf_op jit(solution)/shard_map/ppermute | solution.py:457
  163.7 8.3 %collective-permute-start.13 = (bf16[1056,128]{1,0:T(8,128)(2,1)S(1)}, bf16[1056,128]{1,0:T(8,128)(2,1)S(1)}, u32[]{:S(2)}, u32[]{:S(2)}) collective-permute-start(bf16[1056,128]{1,0:T(8,128)(2,1)S(1)} %get-tuple-element.51), channel_id=1, source_target_pairs={{0,192},{64,0},{128,64},{192,128},{1,193},{65,1},{129,65},{193,129... | collective-permute-start | bytes 811016 | tf_op jit(solution)/shard_map/ppermute | solution.py:458
  167.6 11.1 %collective-permute-start.9 = (bf16[2112,128]{1,0:T(8,128)(2,1)S(1)}, bf16[2112,128]{1,0:T(8,128)(2,1)S(1)}, u32[]{:S(2)}, u32[]{:S(2)}) collective-permute-start(bf16[2112,128]{1,0:T(8,128)(2,1)S(1)} %get-tuple-element.43), channel_id=1, source_target_pairs={{0,32},{32,0},{1,33},{33,1},{2,34},{34,2},{3,35},{35,3},{4,36},{36... | collective-permute-start | bytes 1622024 | tf_op jit(solution)/shard_map/ppermute | solution.py:465
  172.1 10.6 %collective-permute-start.14 = (bf16[1056,128]{1,0:T(8,128)(2,1)S(1)}, bf16[1056,128]{1,0:T(8,128)(2,1)S(1)}, u32[]{:S(2)}, u32[]{:S(2)}) collective-permute-start(bf16[1056,128]{1,0:T(8,128)(2,1)S(1)} %get-tuple-element.52), channel_id=1, source_target_pairs={{0,64},{64,128},{128,192},{192,0},{1,65},{65,129},{129,193},{193,1... | collective-permute-start | bytes 811016 | tf_op jit(solution)/shard_map/ppermute | solution.py:467
  173.6 9.4 %collective-permute-start.17 = (bf16[1056,128]{1,0:T(8,128)(2,1)S(1)}, bf16[1056,128]{1,0:T(8,128)(2,1)S(1)}, u32[]{:S(2)}, u32[]{:S(2)}) collective-permute-start(bf16[1056,128]{1,0:T(8,128)(2,1)S(1)} %get-tuple-element.55), channel_id=1, source_target_pairs={{0,192},{64,0},{128,64},{192,128},{1,193},{65,1},{129,65},{193,129... | collective-permute-start | bytes 811016 | tf_op jit(solution)/shard_map/ppermute | solution.py:468
  175.4 11.4 %collective-permute-start.15 = (bf16[1056,128]{1,0:T(8,128)(2,1)S(1)}, bf16[1056,128]{1,0:T(8,128)(2,1)S(1)}, u32[]{:S(2)}, u32[]{:S(2)}) collective-permute-start(bf16[1056,128]{1,0:T(8,128)(2,1)S(1)} %get-tuple-element.53), channel_id=1, source_target_pairs={{0,64},{64,128},{128,192},{192,0},{1,65},{65,129},{129,193},{193,1... | collective-permute-start | bytes 811016 | tf_op jit(solution)/shard_map/ppermute | solution.py:460
  175.7 11.2 %collective-permute-start.16 = (bf16[1056,128]{1,0:T(8,128)(2,1)S(1)}, bf16[1056,128]{1,0:T(8,128)(2,1)S(1)}, u32[]{:S(2)}, u32[]{:S(2)}) collective-permute-start(bf16[1056,128]{1,0:T(8,128)(2,1)S(1)} %get-tuple-element.54), channel_id=1, source_target_pairs={{0,192},{64,0},{128,64},{192,128},{1,193},{65,1},{129,65},{193,129... | collective-permute-start | bytes 811016 | tf_op jit(solution)/shard_map/ppermute | solution.py:461
  (5 other events, 151.4 us)

commit v2 on v1

--- a/solution.py
+++ b/solution.py
@@ -157,10 +157,10 @@
 
 
 def forward_body(
-    cap, recv, gate, up, down_h, own_h, own_far_h, other_h, other_far_h, rows, slope, act, middle,
-    ret, down, piece, x_out, slope_out, act_out, middle_out, sems,
+    cap, recv, gate, up_h, down_h, own_h, own_far_h, other_h, other_far_h, rows, slope, act, middle,
+    ret, up, down, piece, x_out, slope_out, act_out, middle_out, sems,
 ):
-    pairs, first_unit = [(down_h, down)], 0
+    pairs, first_unit = [(up_h, up), (down_h, down)], 0
     for source in (own_h, own_far_h, other_h, other_far_h):
         pairs.append((source, piece.at[first_unit : first_unit + source.shape[0]]))
         first_unit += source.shape[0]
@@ -178,7 +178,7 @@
     keep = as_bf16(slot < cap)
     x = recv[...] * jnp.concatenate([keep] * (model // 128), axis=1)
     x_out[...] = x
-    saves = [save(x_out, rows, 5)]
+    saves = [save(x_out, rows, 6)]
     pick = as_bf16(iota((experts, count), 1) == iota((experts, count), 0) * STEP + cap)
     found = nn(pick, recv[:, 0:256]).astype(BF16)
     row = iota((count, experts), 0)
@@ -189,21 +189,22 @@
     mine = jnp.logical_and(iota((count, 128), 1) == slot, slot < cap)
     weight = jnp.sum(jnp.where(mine, wide, 0.0), axis=1, keepdims=True)
     g = nt(gate[...], x)
+    copies[0].wait()
     u = nt(up[...], x)
     s = sigmoid(g)
     a = g * s
     act_out[...] = a
-    saves.append(save(act_out, act, 6))
+    saves.append(save(act_out, act, 7))
     slope_out[...] = u * s * (1.0 + g * (1.0 - s))
-    saves.append(save(slope_out, slope, 7))
+    saves.append(save(slope_out, slope, 8))
     hidden = (a * u).astype(BF16)
     middle_out[...] = hidden
-    saves.append(save(middle_out, middle, 8))
-    copies[0].wait()
+    saves.append(save(middle_out, middle, 9))
+    copies[1].wait()
     acc = weight * tn(hidden, down[...])
     units = piece.shape[1] // 3
     take = lambda i: piece[:, i * units : (i + 1) * units, :].reshape(-1, model)
-    for copy in copies[1:]:
+    for copy in copies[2:]:
         copy.wait()
     a = nt(take(0), x)
     b = nt(take(1), x)
@@ -412,16 +413,17 @@
         [shape((rows, model), BF16), shape((width, rows), F32), shape((width, rows), F32)]
         + [shape((width, rows), BF16), shape((2 * experts * cap, model // 2), BF16)],
         [recv, gate_t, up_t, down, gathered, gathered_far, other, other_far],
-        specs=[VMEM] * 3 + [HBM] * 5,
+        specs=[VMEM] * 2 + [HBM] * 6,
         out_specs=[HBM, HBM, HBM, HBM, VMEM],
         scratch=[
+            weight_buf,
             weight_buf,
             pltpu.VMEM((16,) + shard.shape, BF16),
             pltpu.VMEM((rows, model), BF16),
             pltpu.VMEM((width, rows), F32),
             pltpu.VMEM((width, rows), F32),
             pltpu.VMEM((width, rows), BF16),
-            pltpu.SemaphoreType.DMA((9,)),
+            pltpu.SemaphoreType.DMA((10,)),
         ],
         flops=6 * rows * (width + 768) * model,
         grant=GRANT_F,

time: 190 us -> 190 us (level)
  no operation moved by 1% of the time
where the time goes in v2:
time: 190 us; the launch traced here: 188 us
  blocking collectives  78.9 us (42%)
  waiting for transfers between devices  48.2 us (25%)
  starting transfers between devices  31.7 us (17%)
  Pallas kernels  28.4 us (15%)
    all_to_all x2, blocking collectives, exchange(): out = lax.all_to_all(v, EXPERT, 0, 0, tiled=True)  78.9 us
    pallas_call x10, Pallas kernels, call(): pl.pallas_call(body, out_shape=tuple(outs), in_specs=specs or [VMEM] * le...  28.4 us
    ppermute x7, waiting for transfers between devices, shift(): return lax.ppermute(v, axis, [(s, (s + by) % size) for s in range(size)])  27.8 us
    all_to_all x1, starting transfers between devices, exchange(): out = lax.all_to_all(v, EXPERT, 0, 0, tiled=True)  11.9 us
    ppermute x7, starting transfers between devices, shift(): return lax.ppermute(v, axis, [(s, (s + by) % size) for s in range(size)])  8.87 us
    ppermute x1, waiting for transfers between devices, on_device(): late_up = lax.ppermute(late_up, 'x', up)  4.08 us
    ppermute x1, waiting for transfers between devices, on_device(): a = lax.ppermute(far_up, 'x', up)  4.02 us
    ppermute x1, waiting for transfers between devices, on_device(): now_up = lax.ppermute(up_now, 'x', up)  3.86 us
  transfers between devices with their start and end apart: 19, of which 10 were waited for; matrix products, arithmetic and copies ran while one was open for 0% of the time, Pallas kernels for 1%

profile of v2, /device:TPU:8, one launch (start us, length us, event | category | flops | bytes accessed | tf_op | source)
XLA Modules:
  0.0 188.3 jit_solution(11313362163159439185)
XLA Ops:
  0.6 4.5 %shard_map.121 = (bf16[768,1024]{1,0:T(8,128)(2,1)}, f32[4,128]{1,0:T(4,128)}, bf16[144,1024]{1,0:T(8,128)(2,1)}) custom-call(bf16[128,1024]{1,0:T(8,128)(2,1)} %tok_h.1, f32[32,1024]{1,0:T(8,128)} %bitcast.59, s32[4,128]{1,0:T(4,128)} %bitcast.46, s32[4,128]{1,0:T(4,128)} %bitcast.48, bf16[86,1024]{1,0:T(8,128)(2,1)} %bitcast.57, ...), custom_call_target="tpu_custom_call" | custom-call | flops 402653184 | bytes 2795520 | tf_op jit(solution)/shard_map/pallas_call | solution.py:26
  5.2 2.0 %collective-permute-start = (bf16[144,1024]{1,0:T(8,128)(2,1)}, bf16[144,1024]{1,0:T(8,128)(2,1)S(1)}, u32[]{:S(2)}, u32[]{:S(2)}) collective-permute-start(bf16[144,1024]{1,0:T(8,128)(2,1)} %get-tuple-element.32), channel_id=1, source_target_pairs={{0,4},{4,0},{1,5},{5,1},{2,6},{6,2},{3,7},{7,3},{8,12},{12,8},{9,1... | collective-permute-start | bytes 884744 | tf_op jit(solution)/shard_map/ppermute | solution.py:388
  7.6 1.6 collective-permute-start.1
  9.2 11.9 %all-to-all-start = ((bf16[32,24,1024]{2,1,0:T(8,128)(2,1)}), bf16[32,24,1024]{2,1,0:T(8,128)(2,1)}, u32[]{:S(2)}, u32[]{:S(2)}) async-start(bf16[32,24,1024]{2,1,0:T(8,128)(2,1)} %bitcast.50), calls=%async_computation | async-start | bytes 3145728 | tf_op jit(solution)/shard_map/all_to_all | solution.py:402
  21.5 1.7 collective-permute-start.3
  23.3 12.8 %collective-permute-done.3 = bf16[144,1024]{1,0:T(8,128)(2,1)S(1)} collective-permute-done((bf16[144,1024]{1,0:T(8,128)(2,1)S(1)}, bf16[144,1024]{1,0:T(8,128)(2,1)S(1)}, u32[]{:S(2)}, u32[]{:S(2)}) %collective-permute-start.3) | collective-permute-done | bytes 294944 | tf_op jit(solution)/shard_map/ppermute | solution.py:388
  39.1 13.0 %collective-permute-done.5 = bf16[144,1024]{1,0:T(8,128)(2,1)S(1)} collective-permute-done((bf16[144,1024]{1,0:T(8,128)(2,1)S(1)}, bf16[144,1024]{1,0:T(8,128)(2,1)S(1)}, u32[]{:S(2)}, u32[]{:S(2)}) %collective-permute-start.5) | collective-permute-done | bytes 294944 | tf_op jit(solution)/shard_map/ppermute | solution.py:388
  52.1 2.0 %collective-permute-done.6 = bf16[144,1024]{1,0:T(8,128)(2,1)S(1)} collective-permute-done((bf16[144,1024]{1,0:T(8,128)(2,1)S(1)}, bf16[144,1024]{1,0:T(8,128)(2,1)S(1)}, u32[]{:S(2)}, u32[]{:S(2)}) %collective-permute-start.6) | collective-permute-done | bytes 294944 | tf_op jit(solution)/shard_map/ppermute | solution.py:388
  54.4 2.0 %collective-permute-done.8.other_far_h = bf16[2,144,1024]{2,1,0:T(8,128)(2,1)S(1)} collective-permute-done((bf16[2,144,1024]{2,1,0:T(8,128)(2,1)S(1)}, bf16[2,144,1024]{2,1,0:T(8,128)(2,1)S(1)}, u32[]{:S(2)}, u32[]{:S(2)}) %collective-permute-start.8) | collective-permute-done | bytes 589856 | tf_op jit(solution)/shard_map/ppermute | solution.py:410
  56.4 3.2 %all-to-all-done = bf16[32,24,1024]{2,1,0:T(8,128)(2,1)} async-done(((bf16[32,24,1024]{2,1,0:T(8,128)(2,1)}), bf16[32,24,1024]{2,1,0:T(8,128)(2,1)}, u32[]{:S(2)}, u32[]{:S(2)}) %all-to-all-start) | async-done | bytes 1572896 | tf_op jit(solution)/shard_map/all_to_all | solution.py:402
  59.6 11.2 %shard_map.122 = (bf16[768,1024]{1,0:T(8,128)(2,1)}, f32[704,768]{1,0:T(8,128)}, f32[704,768]{1,0:T(8,128)}, bf16[704,768]{1,0:T(8,128)(2,1)S(1)}, bf16[1280,512]{1,0:T(8,128)(2,1)S(1)}) custom-call(bf16[768,1024]{1,0:T(8,128)(2,1)} %bitcast.6.recv, bf16[704,1024]{1,0:T(8,128)(2,1)S(1)} %bitcast.45, bf16[704,1024]{1,0:T(8,128)(2,1)} %bitcast.53, ...), custom_call_target="tpu_custom_call" | custom-call | flops 6945767424 | bytes 18907136 | tf_op jit(solution)/shard_map/pallas_call | solution.py:26
  70.8 40.3 %all_to_all.15 = bf16[32,40,512]{2,1,0:T(8,128)(2,1)S(1)} all-to-all(bf16[32,40,512]{2,1,0:T(8,128)(2,1)S(1)} %bitcast.42), channel_id=1, replica_groups=mesh['x'=4,'core'=2,'zq'=4,'zp'=2,'y'=4] {'zq','zp','y'}, dimensions={0} | all-to-all | bytes 2621440 | tf_op jit(solution)/shard_map/all_to_all | solution.py:402
  111.2 2.7 %shard_map.123 = bf16[1280,512]{1,0:T(8,128)(2,1)S(1)} custom-call(bf16[1280,512]{1,0:T(8,128)(2,1)S(1)} %bitcast.43, f32[4,128]{1,0:T(4,128)S(1)} %copy-done.7, s32[4,128]{1,0:T(4,128)S(1)} %bitcast.47, s32[4,128]{1,0:T(4,128)S(1)} %bitcast.49), custom_call_target="tpu_custom_call" | custom-call | flops 805306368 | bytes 2627584 | tf_op jit(solution)/shard_map/pallas_call | solution.py:26
  113.9 38.6 %all_to_all.16 = bf16[32,40,512]{2,1,0:T(8,128)(2,1)S(1)} all-to-all(bf16[32,40,512]{2,1,0:T(8,128)(2,1)S(1)} %bitcast.44), channel_id=1, replica_groups=mesh['x'=4,'core'=2,'zq'=4,'zp'=2,'y'=4] {'zq','zp','y'}, dimensions={0} | all-to-all | bytes 2621440 | tf_op jit(solution)/shard_map/all_to_all | solution.py:402
  152.5 3.7 %shard_map.124 = (bf16[704,768]{1,0:T(8,128)(2,1)S(1)}, bf16[704,768]{1,0:T(8,128)(2,1)S(1)}, bf16[768,1024]{1,0:T(8,128)(2,1)S(1)}, bf16[2112,128]{1,0:T(8,128)(2,1)S(1)}, bf16[2112,128]{1,0:T(8,128)(2,1)S(1)}) custom-call(bf16[1280,512]{1,0:T(8,128)(2,1)S(1)} %bitcast.39, bf16[768,1024]{1,0:T(8,128)(2,1)S(1)} %copy-done, f32[704,768]{1,0:T(8,128)S(1)} %copy-done.1, ...), custom_call_target="tpu_custom_call" | custom-call | flops 2214592512 | bytes 14548992 | tf_op jit(solution)/shard_map/pallas_call | solution.py:26
  156.2 2.6 %shard_map.126 = (bf16[2,2112,128]{2,1,0:T(8,128)(2,1)S(1)}, bf16[2,2112,128]{2,1,0:T(8,128)(2,1)S(1)}) custom-call(bf16[704,768]{1,0:T(8,128)(2,1)S(1)} %get-tuple-element.39.d_gate, bf16[704,768]{1,0:T(8,128)(2,1)S(1)} %get-tuple-element.40.d_up, bf16[704,768]{1,0:T(8,128)(2,1)S(1)} %get-tuple-element.38.hidden, bf16[768,1024]{1,0:T(8,128)(2,1)S(1)} %copy-done, ...), custom_call_target="tpu_custom_call" | custom-call | flops 1660944384 | bytes 8552448 | tf_op jit(solution)/shard_map/pallas_call | solution.py:26
  159.4 3.0 %collective-permute-done.11.got = bf16[2112,128]{1,0:T(8,128)(2,1)S(1)} collective-permute-done((bf16[2112,128]{1,0:T(8,128)(2,1)S(1)}, bf16[2112,128]{1,0:T(8,128)(2,1)S(1)}, u32[]{:S(2)}, u32[]{:S(2)}) %collective-permute-start.11) | collective-permute-done | bytes 540704 | tf_op jit(solution)/shard_map/ppermute | solution.py:450
  164.1 1.8 collective-permute-start.13
  165.8 2.1 %shard_map.125 = (bf16[2112,128]{1,0:T(8,128)(2,1)S(1)}, bf16[2112,128]{1,0:T(8,128)(2,1)S(1)}) custom-call(bf16[704,768]{1,0:T(8,128)(2,1)S(1)} %get-tuple-element.39.d_gate, bf16[704,768]{1,0:T(8,128)(2,1)S(1)} %get-tuple-element.40.d_up, bf16[704,768]{1,0:T(8,128)(2,1)S(1)} %get-tuple-element.38.hidden, bf16[768,1024]{1,0:T(8,128)(2,1)S(1)} %copy-done, ...), custom_call_target="tpu_custom_call" | custom-call | flops 830472192 | bytes 7471104 | tf_op jit(solution)/shard_map/pallas_call | solution.py:26
  168.3 4.0 %collective-permute-done.12.b = bf16[1056,128]{1,0:T(8,128)(2,1)S(1)} collective-permute-done((bf16[1056,128]{1,0:T(8,128)(2,1)S(1)}, bf16[1056,128]{1,0:T(8,128)(2,1)S(1)}, u32[]{:S(2)}, u32[]{:S(2)}) %collective-permute-start.12) | collective-permute-done | bytes 270368 | tf_op jit(solution)/shard_map/ppermute | solution.py:459
  174.0 1.8 collective-permute-start.17
  176.0 3.0 %collective-permute-start.16 = (bf16[1056,128]{1,0:T(8,128)(2,1)S(1)}, bf16[1056,128]{1,0:T(8,128)(2,1)S(1)}, u32[]{:S(2)}, u32[]{:S(2)}) collective-permute-start(bf16[1056,128]{1,0:T(8,128)(2,1)S(1)} %get-tuple-element.54), channel_id=1, source_target_pairs={{0,192},{64,0},{128,64},{192,128},{1,193},{65,1},{129,65},{193,129... | collective-permute-start | bytes 811016 | tf_op jit(solution)/shard_map/ppermute | solution.py:463
  179.0 4.1 %collective-permute-done.14.up_late = bf16[1056,128]{1,0:T(8,128)(2,1)S(1)} collective-permute-done((bf16[1056,128]{1,0:T(8,128)(2,1)S(1)}, bf16[1056,128]{1,0:T(8,128)(2,1)S(1)}, u32[]{:S(2)}, u32[]{:S(2)}) %collective-permute-start.14) | collective-permute-done | bytes 270368 | tf_op jit(solution)/shard_map/ppermute | solution.py:469
  183.3 3.9 %collective-permute-done.15.up_now = bf16[1056,128]{1,0:T(8,128)(2,1)S(1)} collective-permute-done((bf16[1056,128]{1,0:T(8,128)(2,1)S(1)}, bf16[1056,128]{1,0:T(8,128)(2,1)S(1)}, u32[]{:S(2)}, u32[]{:S(2)}) %collective-permute-start.15) | collective-permute-done | bytes 270368 | tf_op jit(solution)/shard_map/ppermute | solution.py:462
  (53 shorter events, 10.1 us)
Async XLA Ops:
  5.2 16.0 %collective-permute-start = (bf16[144,1024]{1,0:T(8,128)(2,1)}, bf16[144,1024]{1,0:T(8,128)(2,1)S(1)}, u32[]{:S(2)}, u32[]{:S(2)}) collective-permute-start(bf16[144,1024]{1,0:T(8,128)(2,1)} %get-tuple-element.32), channel_id=1, source_target_pairs={{0,4},{4,0},{1,5},{5,1},{2,6},{6,2},{3,7},{7,3},{8,12},{12,8},{9,1... | collective-permute-start | bytes 884744 | tf_op jit(solution)/shard_map/ppermute | solution.py:388
  7.2 16.1 %collective-permute-start.2 = (bf16[144,1024]{1,0:T(8,128)(2,1)}, bf16[144,1024]{1,0:T(8,128)(2,1)S(1)}, u32[]{:S(2)}, u32[]{:S(2)}) collective-permute-start(bf16[144,1024]{1,0:T(8,128)(2,1)} %get-tuple-element.32), channel_id=1, source_target_pairs={{0,3},{1,0},{2,1},{3,2},{4,7},{5,4},{6,5},{7,6},{8,11},{9,8},{10,9... | collective-permute-start | bytes 884744 | tf_op jit(solution)/shard_map/ppermute | solution.py:388
  7.6 15.7 %collective-permute-start.1 = (bf16[144,1024]{1,0:T(8,128)(2,1)}, bf16[144,1024]{1,0:T(8,128)(2,1)S(1)}, u32[]{:S(2)}, u32[]{:S(2)}) collective-permute-start(bf16[144,1024]{1,0:T(8,128)(2,1)} %get-tuple-element.32), channel_id=1, source_target_pairs={{0,1},{1,2},{2,3},{3,0},{4,5},{5,6},{6,7},{7,4},{8,9},{9,10},{10,1... | collective-permute-start | bytes 884744 | tf_op jit(solution)/shard_map/ppermute | solution.py:388
  9.2 50.4 %all-to-all-start = ((bf16[32,24,1024]{2,1,0:T(8,128)(2,1)}), bf16[32,24,1024]{2,1,0:T(8,128)(2,1)}, u32[]{:S(2)}, u32[]{:S(2)}) async-start(bf16[32,24,1024]{2,1,0:T(8,128)(2,1)} %bitcast.50), calls=%async_computation | async-start | bytes 3145728 | tf_op jit(solution)/shard_map/all_to_all | solution.py:402
  21.1 15.1 %collective-permute-start.4 = (bf16[144,1024]{1,0:T(8,128)(2,1)S(1)}, bf16[144,1024]{1,0:T(8,128)(2,1)S(1)}, u32[]{:S(2)}, u32[]{:S(2)}) collective-permute-start(bf16[144,1024]{1,0:T(8,128)(2,1)S(1)} %collective-permute-done), channel_id=1, source_target_pairs={{0,3},{1,0},{2,1},{3,2},{4,7},{5,4},{6,5},{7,6},{8,11},{9,8},{10,9... | collective-permute-start | bytes 884744 | tf_op jit(solution)/shard_map/ppermute | solution.py:388
  21.5 14.7 %collective-permute-start.3 = (bf16[144,1024]{1,0:T(8,128)(2,1)S(1)}, bf16[144,1024]{1,0:T(8,128)(2,1)S(1)}, u32[]{:S(2)}, u32[]{:S(2)}) collective-permute-start(bf16[144,1024]{1,0:T(8,128)(2,1)S(1)} %collective-permute-done), channel_id=1, source_target_pairs={{0,1},{1,2},{2,3},{3,0},{4,5},{5,6},{6,7},{7,4},{8,9},{9,10},{10,1... | collective-permute-start | bytes 884744 | tf_op jit(solution)/shard_map/ppermute | solution.py:388
  36.3 20.1 %collective-permute-start.7 = (bf16[6,144,1024]{2,1,0:T(8,128)(2,1)S(1)}, bf16[6,144,1024]{2,1,0:T(8,128)(2,1)}, u32[]{:S(2)}, u32[]{:S(2)}) collective-permute-start(bf16[6,144,1024]{2,1,0:T(8,128)(2,1)S(1)} %bitcast_dynamic-update-slice_fusion.own_h), channel_id=1, source_target_pairs={{0,32},{32,0},{1,33},{33,1},{2,34},{34,2},{3,35},{35,3},{4,36},{36... | collective-permute-start | bytes 5308424 | tf_op jit(solution)/shard_map/ppermute | solution.py:409
  36.4 15.7 %collective-permute-start.5 = (bf16[144,1024]{1,0:T(8,128)(2,1)S(1)}, bf16[144,1024]{1,0:T(8,128)(2,1)S(1)}, u32[]{:S(2)}, u32[]{:S(2)}) collective-permute-start(bf16[144,1024]{1,0:T(8,128)(2,1)S(1)} %collective-permute-done.1), channel_id=1, source_target_pairs={{0,1},{1,2},{2,3},{3,0},{4,5},{5,6},{6,7},{7,4},{8,9},{9,10},{10,1... | collective-permute-start | bytes 884744 | tf_op jit(solution)/shard_map/ppermute | solution.py:388
  37.8 16.2 %collective-permute-start.6 = (bf16[144,1024]{1,0:T(8,128)(2,1)S(1)}, bf16[144,1024]{1,0:T(8,128)(2,1)S(1)}, u32[]{:S(2)}, u32[]{:S(2)}) collective-permute-start(bf16[144,1024]{1,0:T(8,128)(2,1)S(1)} %collective-permute-done.4), channel_id=1, source_target_pairs={{0,3},{1,0},{2,1},{3,2},{4,7},{5,4},{6,5},{7,6},{8,11},{9,8},{10,9... | collective-permute-start | bytes 884744 | tf_op jit(solution)/shard_map/ppermute | solution.py:388
  54.1 2.3 %collective-permute-start.8 = (bf16[2,144,1024]{2,1,0:T(8,128)(2,1)S(1)}, bf16[2,144,1024]{2,1,0:T(8,128)(2,1)S(1)}, u32[]{:S(2)}, u32[]{:S(2)}) collective-permute-start(bf16[2,144,1024]{2,1,0:T(8,128)(2,1)S(1)} %pad_maximum_fusion.own_far_h), channel_id=1, source_target_pairs={{0,32},{32,0},{1,33},{33,1},{2,34},{34,2},{3,35},{35,3},{4,36},{36... | collective-permute-start | bytes 1769480 | tf_op jit(solution)/shard_map/ppermute | solution.py:410
  70.8 40.4 %copy-start.5 = (s32[128,4]{0,1:T(4,128)S(1)}, s32[128,4]{0,1:T(4,128)}, u32[]{:S(2)}) copy-start(s32[128,4]{0,1:T(4,128)} %param.12) | copy-start | bytes 6148
  70.8 40.4 %copy-start.6 = (s32[128,4]{0,1:T(4,128)S(1)}, s32[128,4]{0,1:T(4,128)}, u32[]{:S(2)}) copy-start(s32[128,4]{0,1:T(4,128)} %param.13) | copy-start | bytes 6148
  70.8 81.6 %copy-start.2 = (f32[704,768]{1,0:T(8,128)S(1)}, f32[704,768]{1,0:T(8,128)}, u32[]{:S(2)}) copy-start(f32[704,768]{1,0:T(8,128)} %get-tuple-element.37.act) | copy-start | bytes 6488068
  111.1 41.3 %copy-start.1 = (f32[704,768]{1,0:T(8,128)S(1)}, f32[704,768]{1,0:T(8,128)}, u32[]{:S(2)}) copy-start(f32[704,768]{1,0:T(8,128)} %get-tuple-element.36.slope) | copy-start | bytes 6488068
  111.2 41.3 %copy-start.3 = (bf16[1,704,1024]{2,1,0:T(8,128)(2,1)S(1)}, bf16[1,704,1024]{2,1,0:T(8,128)(2,1)}, u32[]{:S(2)}) copy-start(bf16[1,704,1024]{2,1,0:T(8,128)(2,1)} %param.19) | copy-start | bytes 4325380
  158.8 9.2 %collective-permute-start.10 = (bf16[2,2112,128]{2,1,0:T(8,128)(2,1)S(1)}, bf16[2,2112,128]{2,1,0:T(8,128)(2,1)S(1)}, u32[]{:S(2)}, u32[]{:S(2)}) collective-permute-start(bf16[2,2112,128]{2,1,0:T(8,128)(2,1)S(1)} %get-tuple-element.45), channel_id=1, source_target_pairs={{0,32},{32,0},{1,33},{33,1},{2,34},{34,2},{3,35},{35,3},{4,36},{36... | collective-permute-start | bytes 3244040 | tf_op jit(solution)/shard_map/ppermute | solution.py:453
  158.9 3.5 %collective-permute-start.11 = (bf16[2112,128]{1,0:T(8,128)(2,1)S(1)}, bf16[2112,128]{1,0:T(8,128)(2,1)S(1)}, u32[]{:S(2)}, u32[]{:S(2)}) collective-permute-start(bf16[2112,128]{1,0:T(8,128)(2,1)S(1)} %get-tuple-element.48), channel_id=1, source_target_pairs={{0,32},{32,0},{1,33},{33,1},{2,34},{34,2},{3,35},{35,3},{4,36},{36... | collective-permute-start | bytes 1622024 | tf_op jit(solution)/shard_map/ppermute | solution.py:450
  162.5 9.8 %collective-permute-start.12 = (bf16[1056,128]{1,0:T(8,128)(2,1)S(1)}, bf16[1056,128]{1,0:T(8,128)(2,1)S(1)}, u32[]{:S(2)}, u32[]{:S(2)}) collective-permute-start(bf16[1056,128]{1,0:T(8,128)(2,1)S(1)} %get-tuple-element.49), channel_id=1, source_target_pairs={{0,64},{64,128},{128,192},{192,0},{1,65},{65,129},{129,193},{193,1... | collective-permute-start | bytes 811016 | tf_op jit(solution)/shard_map/ppermute | solution.py:459
  164.1 8.3 %collective-permute-start.13 = (bf16[1056,128]{1,0:T(8,128)(2,1)S(1)}, bf16[1056,128]{1,0:T(8,128)(2,1)S(1)}, u32[]{:S(2)}, u32[]{:S(2)}) collective-permute-start(bf16[1056,128]{1,0:T(8,128)(2,1)S(1)} %get-tuple-element.51), channel_id=1, source_target_pairs={{0,192},{64,0},{128,64},{192,128},{1,193},{65,1},{129,65},{193,129... | collective-permute-start | bytes 811016 | tf_op jit(solution)/shard_map/ppermute | solution.py:460
  167.9 11.1 %collective-permute-start.9 = (bf16[2112,128]{1,0:T(8,128)(2,1)S(1)}, bf16[2112,128]{1,0:T(8,128)(2,1)S(1)}, u32[]{:S(2)}, u32[]{:S(2)}) collective-permute-start(bf16[2112,128]{1,0:T(8,128)(2,1)S(1)} %get-tuple-element.43), channel_id=1, source_target_pairs={{0,32},{32,0},{1,33},{33,1},{2,34},{34,2},{3,35},{35,3},{4,36},{36... | collective-permute-start | bytes 1622024 | tf_op jit(solution)/shard_map/ppermute | solution.py:467
  172.4 10.6 %collective-permute-start.14 = (bf16[1056,128]{1,0:T(8,128)(2,1)S(1)}, bf16[1056,128]{1,0:T(8,128)(2,1)S(1)}, u32[]{:S(2)}, u32[]{:S(2)}) collective-permute-start(bf16[1056,128]{1,0:T(8,128)(2,1)S(1)} %get-tuple-element.52), channel_id=1, source_target_pairs={{0,64},{64,128},{128,192},{192,0},{1,65},{65,129},{129,193},{193,1... | collective-permute-start | bytes 811016 | tf_op jit(solution)/shard_map/ppermute | solution.py:469
  174.0 9.4 %collective-permute-start.17 = (bf16[1056,128]{1,0:T(8,128)(2,1)S(1)}, bf16[1056,128]{1,0:T(8,128)(2,1)S(1)}, u32[]{:S(2)}, u32[]{:S(2)}) collective-permute-start(bf16[1056,128]{1,0:T(8,128)(2,1)S(1)} %get-tuple-element.55), channel_id=1, source_target_pairs={{0,192},{64,0},{128,64},{192,128},{1,193},{65,1},{129,65},{193,129... | collective-permute-start | bytes 811016 | tf_op jit(solution)/shard_map/ppermute | solution.py:470
  175.8 11.4 %collective-permute-start.15 = (bf16[1056,128]{1,0:T(8,128)(2,1)S(1)}, bf16[1056,128]{1,0:T(8,128)(2,1)S(1)}, u32[]{:S(2)}, u32[]{:S(2)}) collective-permute-start(bf16[1056,128]{1,0:T(8,128)(2,1)S(1)} %get-tuple-element.53), channel_id=1, source_target_pairs={{0,64},{64,128},{128,192},{192,0},{1,65},{65,129},{129,193},{193,1... | collective-permute-start | bytes 811016 | tf_op jit(solution)/shard_map/ppermute | solution.py:462
  176.0 11.2 %collective-permute-start.16 = (bf16[1056,128]{1,0:T(8,128)(2,1)S(1)}, bf16[1056,128]{1,0:T(8,128)(2,1)S(1)}, u32[]{:S(2)}, u32[]{:S(2)}) collective-permute-start(bf16[1056,128]{1,0:T(8,128)(2,1)S(1)} %get-tuple-element.54), channel_id=1, source_target_pairs={{0,192},{64,0},{128,64},{192,128},{1,193},{65,1},{129,65},{193,129... | collective-permute-start | bytes 811016 | tf_op jit(solution)/shard_map/ppermute | solution.py:463
  (5 other events, 151.4 us)
